TPU v7x, 32 devices: a whole 2x2x4 slice. The times are simulated.
32 devices in a mesh: il: 16 (over z, y, core), xl: 2 (over x).
Axes of the slice: x: 2, y: 2, z: 4, core: 2. Of those that a mesh axis runs over, the one named last changes fastest.
Arguments:
- solution: float32 [64, 128, 512], P('il', 'xl'), may hold values from -6 to 6
- residual: float32 [64, 128, 512], P('il', 'xl'), may hold values from -30 to 30
- direction: float32 [64, 128, 512], P('il', 'xl'), may hold values from -30 to 30
- slope_il: float32 [64, 128, 512], P('il', 'xl'), may hold values from -1.5 to 1.5
- slope_xl: float32 [64, 128, 512], P('il', 'xl'), may hold values from -1.5 to 1.5
- weights: float32 [64, 128, 512], P('il', 'xl'), may hold values from 0.2 to 1
Outputs:
- new_solution: float32 [64, 128, 512], P('il', 'xl')
- new_residual: float32 [64, 128, 512], P('il', 'xl')
- new_direction: float32 [64, 128, 512], P('il', 'xl')
All inputs are finite; a program needn't handle non-finite values.
Results may differ from a plain program's by a relative error of at most 0.00002.
Values sent between devices are 32-bit elements; how exact they have to be, the bound alone decides.
No kernel may reach another device: no remote copies, remote signals or barrier semaphores. Data moves between devices by JAX's collectives and lax.ppermute only.
A program may use at most 64 MiB of HBM per device.

v0:
```python
import jax
import jax.numpy as jnp
from jax import lax
from jax.experimental import pallas as pl
from jax.experimental.pallas import tpu as pltpu
from jax.sharding import PartitionSpec as P


damping = 0.3
VMEM_LIMIT = 16 * 1024 * 1024


def swap_pairs(sizes, axis, parity):
    n_il, n_xl = sizes
    size, other = (n_il, n_xl) if axis == 0 else (n_xl, n_il)
    pairs, real = [], False
    for a in range(size):
        mate = a + 1 if a % 2 == parity else a - 1
        inside = 0 <= mate < size
        real = real or inside
        for b in range(other):
            if inside:
                a_to, b_to = mate, b
            else:
                a_to, b_to = a, (b ^ 1 if (b ^ 1) < other else b)
            here, there = ((a, b), (a_to, b_to)) if axis == 0 else ((b, a), (b_to, a_to))
            pairs.append((here[0] * n_xl + here[1], there[0] * n_xl + there[1]))
    return pairs, real


def time_diff(field):
    steps = field.shape[-1]
    at = lax.broadcasted_iota(jnp.int32, field.shape, field.ndim - 1)
    after = jnp.where(at == steps - 1, 0.0, pltpu.roll(field, steps - 1, field.ndim - 1))
    before = jnp.where(at == 0, 0.0, pltpu.roll(field, 1, field.ndim - 1))
    return 0.5 * (after - before)


def params():
    return pltpu.CompilerParams(vmem_limit_bytes=VMEM_LIMIT)


VMEM = pl.BlockSpec(memory_space=pltpu.VMEM)
HBM = pl.BlockSpec(memory_space=pltpu.HBM)


def f32(*shape):
    return jax.ShapeDtypeStruct(shape, jnp.float32)


def make_pick(rows, cols, steps):
    def kernel(u_hbm, w_hbm, out_ref, sem):
        low = lax.axis_index("il") % 2 == 1

        @pl.when(low)
        def _():
            copy = pltpu.make_async_copy(w_hbm.at[rows - 1], out_ref, sem)
            copy.start()
            copy.wait()

        @pl.when(jnp.logical_not(low))
        def _():
            copy = pltpu.make_async_copy(u_hbm.at[0], out_ref, sem)
            copy.start()
            copy.wait()

    return pl.pallas_call(
        kernel,
        in_specs=[HBM, HBM],
        out_specs=VMEM,
        out_shape=f32(cols, steps),
        scratch_shapes=[pltpu.SemaphoreType.DMA],
        compiler_params=params(),
        name="pick",
    )


def make_pack(rows, cols, steps, xl_parities):
    edge = min(8, cols)

    def kernel(_, u_hbm, sil_hbm, sxl_hbm, w_hbm, g_ref, even_ref, *rest):
        bufs = rest[: len(xl_parities)]
        u_low, s_low, u_cl, s_cl, w_cl, u_cu, sems = rest[len(xl_parities) :]
        il_odd = lax.axis_index("il") % 2
        xl_odd = lax.axis_index("xl") % 2
        last, first = pl.ds(cols - edge, edge), pl.ds(0, edge)
        copies = [
            pltpu.make_async_copy(src, dst, sems.at[k])
            for k, (src, dst) in enumerate(
                (
                    (u_hbm.at[rows - 1], u_low),
                    (sil_hbm.at[rows - 1], s_low),
                    (u_hbm.at[:, last], u_cl),
                    (sxl_hbm.at[:, last], s_cl),
                    (w_hbm.at[:, last], w_cl),
                    (u_hbm.at[:, first], u_cu),
                )
            )
        ]
        for copy in copies:
            copy.start()
        own = [(0, w_hbm.at[rows - 1]), (1, u_hbm.at[0])]
        for parity, src in own:

            @pl.when(il_odd == parity)
            def _(src=src):
                pltpu.make_async_copy(src, even_ref, sems.at[6]).start()

        for copy in copies[:2]:
            copy.wait()
        u = u_low[...]
        g = u + s_low[...] * time_diff(u)
        g_ref[...] = g
        for copy in copies[2:]:
            copy.wait()
        u = u_cl[:, edge - 1, :]
        g = u + s_cl[:, edge - 1, :] * time_diff(u)
        for parity, buf in zip(xl_parities, bufs):
            buf[pl.ds(rows, rows)] = g

            @pl.when(xl_odd == parity)
            def _(buf=buf):
                buf[pl.ds(0, rows)] = w_cl[:, edge - 1, :]

            @pl.when(xl_odd != parity)
            def _(buf=buf):
                buf[pl.ds(0, rows)] = u_cu[:, 0, :]

        for parity, src in own:

            @pl.when(il_odd == parity)
            def _(src=src):
                pltpu.make_async_copy(src, even_ref, sems.at[6]).wait()

    outs = [f32(cols, steps), f32(cols, steps)] + [f32(2 * rows, steps)] * len(xl_parities)
    return pl.pallas_call(
        kernel,
        in_specs=[pl.BlockSpec(memory_space=pl.ANY)] + [HBM] * 4,
        out_specs=[VMEM] * len(outs),
        out_shape=outs,
        scratch_shapes=[pltpu.VMEM((cols, steps), jnp.float32)] * 2
        + [pltpu.VMEM((rows, edge, steps), jnp.float32)] * 4
        + [pltpu.SemaphoreType.DMA((7,))],
        compiler_params=params(),
        name="pack",
    )


def add_products(sums, u, r, image):
    return [s + a * b for s, (a, b) in zip(sums, ((u, image), (r, image), (image, image)))]


def make_inner(rows, cols, steps):
    def kernel(u_ref, r_ref, sil_ref, sxl_ref, w_ref, img_ref, sums_ref):
        col = lax.broadcasted_iota(jnp.int32, (cols, steps), 0)
        flux_before = None
        norm = jnp.zeros((8, steps), jnp.float32)
        sums = [norm] * 3
        for i in range(rows):
            u = u_ref[i]
            w2 = w_ref[i] * w_ref[i]
            slope_t = time_diff(u)
            s_xl = sxl_ref[i]
            ahead = pltpu.roll(u, cols - 1, 0)
            flux_xl = jnp.where(col == cols - 1, 0.0, w2 * (ahead - u - s_xl * slope_t))
            behind = jnp.where(col == 0, 0.0, pltpu.roll(flux_xl, 1, 0))
            image = behind - flux_xl + damping * u
            along = s_xl * flux_xl
            if flux_before is not None:
                image = image + flux_before
            if i < rows - 1:
                s_il = sil_ref[i]
                flux_il = w2 * (u_ref[i + 1] - u - s_il * slope_t)
                image = image - flux_il
                along = along + s_il * flux_il
                flux_before = flux_il
            img_ref[i] = image + time_diff(along)
            for j in range(0, cols, 8):
                at = (i, pl.ds(j, 8))
                r = r_ref[at]
                norm = norm + r * r
                if 0 < i < rows - 1 and 0 < j < cols - 8:
                    sums = add_products(sums, u_ref[at], r, img_ref[at])
        for k, value in enumerate([norm] + sums):
            sums_ref[k] = value

    return pl.pallas_call(
        kernel,
        in_specs=[VMEM] * 5,
        out_specs=[VMEM] * 2,
        out_shape=[f32(rows, cols, steps), f32(4, 8, steps)],
        compiler_params=params(),
        name="inner",
    )


def make_edges(rows, cols, steps, n_il, n_xl, xl_parities, n_dev):
    def kernel(u_ref, r_ref, sil_ref, sxl_ref, w_ref, part_ref, sums_ref, mine_ref, even_ref, odd_ref, g_ref, *rest):
        bufs = rest[:-2]
        img_ref, out_ref = rest[-2:]
        il, xl = lax.axis_index("il"), lax.axis_index("xl")

        def low(ahead):
            w = w_ref[rows - 1]
            flux = w * w * (ahead - mine_ref[...])
            img_ref[rows - 1] = part_ref[rows - 1] + (time_diff(sil_ref[rows - 1] * flux) - flux)

        def high(w, g):
            img_ref[0] += w * w * (u_ref[0] - g)

        for i in range(rows):
            img_ref[i] = part_ref[i]

        @pl.when((il % 2 == 0) & (il < n_il - 1))
        def _():
            low(even_ref[...])

        @pl.when((il % 2 == 1) & (il < n_il - 1))
        def _():
            low(odd_ref[...])

        @pl.when((il % 2 == 0) & (il > 0))
        def _():
            high(odd_ref[...], g_ref[...])

        @pl.when(il % 2 == 1)
        def _():
            high(even_ref[...], g_ref[...])

        half = len(xl_parities)
        for parity, mine, got in zip(xl_parities, bufs[:half], bufs[half:]):

            @pl.when((xl % 2 == parity) & (xl < n_xl - 1))
            def _(mine=mine, got=got):
                w = mine[pl.ds(0, rows)]
                flux = w * w * (got[pl.ds(0, rows)] - mine[pl.ds(rows, rows)])
                add = time_diff(sxl_ref[:, cols - 1, :] * flux) - flux
                for i in range(rows):
                    img_ref[i, pl.ds(cols - 1, 1), :] += add[i : i + 1]

            @pl.when((xl % 2 != parity) & (xl > 0))
            def _(got=got):
                w = got[pl.ds(0, rows)]
                add = w * w * (u_ref[:, 0, :] - got[pl.ds(rows, rows)])
                for i in range(rows):
                    img_ref[i, pl.ds(0, 1), :] += add[i : i + 1]

        sums = [sums_ref[k] for k in range(1, 4)]
        for i in range(rows):
            for j in range(0, cols, 8):
                if not (0 < i < rows - 1 and 0 < j < cols - 8):
                    at = (i, pl.ds(j, 8))
                    sums = add_products(sums, u_ref[at], r_ref[at], img_ref[at])
        lane = lax.broadcasted_iota(jnp.int32, (1, 128), 1)
        row = jnp.zeros((1, 128), jnp.float32)
        for k, value in enumerate([sums_ref[0]] + sums):
            value = sum(value[:, j : j + 128] for j in range(128, steps, 128)) + value[:, :128]
            value = jnp.sum(jnp.sum(value, axis=0, keepdims=True), axis=1, keepdims=True)
            row = jnp.where(lane == k, value, row)
        out_ref[...] = jnp.broadcast_to(row, (n_dev, 128))

    return pl.pallas_call(
        kernel,
        in_specs=[VMEM] * (11 + 2 * len(xl_parities)),
        out_specs=[VMEM, VMEM],
        out_shape=[f32(rows, cols, steps), f32(n_dev, 128)],
        input_output_aliases={5: 0},
        compiler_params=params(),
        name="edges",
    )


def make_update(rows, cols, steps):
    def kernel(sums_ref, x_ref, r_ref, u_ref, img_ref, x_hbm, r_hbm, d_hbm, x_out, r_out, d_out, sems):
        total = jnp.sum(sums_ref[...], axis=0, keepdims=True)
        lane = lax.broadcasted_iota(jnp.int32, total.shape, 1)
        norm_old, along, cross, square = (
            jnp.sum(jnp.where(lane == k, total, 0.0), axis=1, keepdims=True) for k in range(4)
        )
        alpha = norm_old / along
        norm_new = norm_old - 2.0 * alpha * cross + alpha * alpha * square
        beta = norm_new / norm_old
        copies = []
        for i in range(rows):
            u = u_ref[i]
            residual = r_ref[i] - alpha * img_ref[i]
            x_out[i] = x_ref[i] + alpha * u
            r_out[i] = residual
            d_out[i] = residual + beta * u
            for k, (src, dst) in enumerate(((x_out, x_hbm), (r_out, r_hbm), (d_out, d_hbm))):
                copy = pltpu.make_async_copy(src.at[i], dst.at[i], sems.at[k, i])
                copy.start()
                copies.append(copy)
        for copy in copies:
            copy.wait()

    return pl.pallas_call(
        kernel,
        in_specs=[VMEM] * 5,
        out_specs=[HBM] * 3,
        out_shape=[f32(rows, cols, steps)] * 3,
        scratch_shapes=[pltpu.VMEM((rows, cols, steps), jnp.float32)] * 3
        + [pltpu.SemaphoreType.DMA((3, rows))],
        compiler_params=params(),
        name="update",
    )


def solution(mesh):
    n_il, n_xl = mesh.shape["il"], mesh.shape["xl"]
    n_dev = n_il * n_xl
    axes = ("il", "xl")
    even_swap, odd_swap = (swap_pairs((n_il, n_xl), 0, parity)[0] for parity in range(2))
    up = [(i, (i + 1) % n_il) for i in range(n_il)]
    xl_swaps = [swap_pairs((n_il, n_xl), 1, parity) for parity in range(2)]
    xl_parities = [parity for parity in range(2) if xl_swaps[parity][1]]

    def step(x, r, u, s_il, s_xl, w):
        rows, cols, steps = u.shape
        stay = [pltpu.with_memory_space_constraint(a, pltpu.HBM) for a in (u, s_il, s_xl, w)]
        picked = make_pick(rows, cols, steps)(stay[0], stay[3])
        odd = lax.ppermute(picked, axes, odd_swap)
        g, first, *xl_sent = make_pack(rows, cols, steps, xl_parities)(picked, *stay)
        g_got = lax.ppermute(g, "il", up)
        xl_got = []
        for p, buf in zip(xl_parities, xl_sent):
            xl_got.append(lax.ppermute(buf, axes, xl_swaps[p][0]))
        even = lax.ppermute(first, axes, even_swap)
        part, sums = make_inner(rows, cols, steps)(u, r, s_il, s_xl, w)
        image, row = make_edges(rows, cols, steps, n_il, n_xl, xl_parities, n_dev)(
            u, r, s_il, s_xl, w, part, sums, g, even, odd, g_got, *xl_sent, *xl_got
        )
        rows_all = lax.all_to_all(row, axes, 0, 0, tiled=True)
        return make_update(rows, cols, steps)(rows_all, x, r, u, image)

    placed = P("il", "xl", None)
    return jax.shard_map(step, mesh=mesh, in_specs=(placed,) * 6, out_specs=(placed,) * 3, check_vma=False)
```

profile of v0, /device:TPU:0, one launch (start us, length us, event | category | flops | bytes accessed | tf_op | source)
XLA Modules:
  0.0 25.3 jit_solution(20486581533677239)
XLA Ops:
  0.6 0.0 copy-start.4
  0.6 1.0 %pick.1._ = f32[64,512]{1,0:T(8,128)S(1)} custom-call(f32[4,64,512]{2,1,0:T(8,128)} %u_ref.5, f32[4,64,512]{2,1,0:T(8,128)} %w_ref.3), custom_call_target="tpu_custom_call" | custom-call | tf_op jit(solution)/shard_map/pick/pallas_call | solution.py:321
  1.6 0.0 copy-start
  1.6 0.0 copy-start.1
  1.7 0.0 copy-start.2
  1.7 0.0 copy-start.3
  1.7 3.0 %collective-permute-start.1 = (f32[64,512]{1,0:T(8,128)S(1)}, f32[64,512]{1,0:T(8,128)S(1)}, u32[]{:S(2)}, u32[]{:S(2)}) collective-permute-start(f32[64,512]{1,0:T(8,128)S(1)} %pick.1._), channel_id=1, source_target_pairs={{0,1},{1,0},{2,4},{3,5},{4,2},{5,3},{6,8},{7,9},{8,6},{9,7},{10,12... | collective-permute-start | bytes 393224 | tf_op jit(solution)/shard_map/ppermute | solution.py:322
  4.7 1.3 %pack.1 = (f32[64,512]{1,0:T(8,128)S(1)}, f32[64,512]{1,0:T(8,128)S(1)}, f32[8,512]{1,0:T(8,128)S(1)}) custom-call(f32[64,512]{1,0:T(8,128)S(1)} %pick.1._, f32[4,64,512]{2,1,0:T(8,128)} %u_ref.5, f32[4,64,512]{2,1,0:T(8,128)} %sil_ref.3, f32[4,64,512]{2,1,0:T(8,128)} %sxl_ref.3, f32[4,64,512]{2,1,0:T(8,128)} %w_ref.3), custom_call_target="tpu_custom_call" | custom-call | tf_op jit(solution)/shard_map/pack/pallas_call | solution.py:323
  6.0 0.2 collective-permute-start
  6.2 0.4 %collective-permute-start.2 = (f32[64,512]{1,0:T(8,128)S(1)}, f32[64,512]{1,0:T(8,128)S(1)}, u32[]{:S(2)}, u32[]{:S(2)}) collective-permute-start(f32[64,512]{1,0:T(8,128)S(1)} %get-tuple-element.12.mine_ref), channel_id=1, source_target_pairs={{0,2},{2,4},{4,6},{6,8},{8,10},{10,12},{12,14},{14,16},{16,18},{18... | collective-permute-start | bytes 393224 | tf_op jit(solution)/shard_map/ppermute | solution.py:324
  6.6 1.2 %collective-permute-start.3 = (f32[8,512]{1,0:T(8,128)S(1)}, f32[8,512]{1,0:T(8,128)S(1)}, u32[]{:S(2)}, u32[]{:S(2)}) collective-permute-start(f32[8,512]{1,0:T(8,128)S(1)} %get-tuple-element.14.rest_0_), channel_id=1, source_target_pairs={{0,1},{2,3},{4,5},{6,7},{8,9},{10,11},{12,13},{14,15},{16,17},{18,... | collective-permute-start | bytes 49160 | tf_op jit(solution)/shard_map/ppermute | solution.py:327
  7.8 0.0 copy-done.4
  7.8 0.0 copy-done
  7.8 0.0 copy-done.1
  7.8 0.0 copy-done.2
  7.8 0.0 copy-done.3
  7.8 1.0 %inner.1 = (f32[4,64,512]{2,1,0:T(8,128)S(1)}, f32[4,8,512]{2,1,0:T(8,128)S(1)}) custom-call(f32[4,64,512]{2,1,0:T(8,128)S(1)} %copy-done, f32[4,64,512]{2,1,0:T(8,128)S(1)} %copy-done.4, f32[4,64,512]{2,1,0:T(8,128)S(1)} %copy-done.2, f32[4,64,512]{2,1,0:T(8,128)S(1)} %copy-done.3, f32[4,64,512]{2,1,0:T(8,128)S(1)} %copy-done.1), custom_call_target="tpu_custom_call" | custom-call | tf_op jit(solution)/shard_map/inner/pallas_call | solution.py:329
  8.8 1.5 %collective-permute-done.3.rest_1_ = f32[8,512]{1,0:T(8,128)S(1)} collective-permute-done((f32[8,512]{1,0:T(8,128)S(1)}, f32[8,512]{1,0:T(8,128)S(1)}, u32[]{:S(2)}, u32[]{:S(2)}) %collective-permute-start.3) | collective-permute-done | bytes 16416 | tf_op jit(solution)/shard_map/ppermute | solution.py:327
  10.3 0.0 collective-permute-done.1.odd_ref
  10.3 0.0 collective-permute-done.even_ref
  10.3 3.0 %collective-permute-done.2.g_ref = f32[64,512]{1,0:T(8,128)S(1)} collective-permute-done((f32[64,512]{1,0:T(8,128)S(1)}, f32[64,512]{1,0:T(8,128)S(1)}, u32[]{:S(2)}, u32[]{:S(2)}) %collective-permute-start.2) | collective-permute-done | bytes 131104 | tf_op jit(solution)/shard_map/ppermute | solution.py:324
  13.3 0.5 %edges.1 = (f32[4,64,512]{2,1,0:T(8,128)S(1)}, f32[32,128]{1,0:T(8,128)S(1)}) custom-call(f32[4,64,512]{2,1,0:T(8,128)S(1)} %copy-done, f32[4,64,512]{2,1,0:T(8,128)S(1)} %copy-done.4, f32[4,64,512]{2,1,0:T(8,128)S(1)} %copy-done.2, f32[4,64,512]{2,1,0:T(8,128)S(1)} %copy-done.3, f32[4,64,512]{2,1,0:T(8,128)S(1)} %copy-done.1, ...), custom_call_target="tpu_custom_call", output_to_operand_aliasing={{0}: (5, {})} | custom-call | tf_op jit(solution)/shard_map/edges/pallas_call | solution.py:330
  13.8 10.1 %all_to_all.11 = f32[32,1,128]{2,1,0:T(1,128)S(1)} all-to-all(f32[32,1,128]{2,1,0:T(1,128)S(1)} %bitcast.5), channel_id=1, replica_groups=mesh['il'=16,'xl'=2] {'il','xl'}, dimensions={0} | all-to-all | bytes 32768 | tf_op jit(solution)/shard_map/all_to_all | solution.py:333
  23.9 1.4 %update.1 = (f32[4,64,512]{2,1,0:T(8,128)}, f32[4,64,512]{2,1,0:T(8,128)}, f32[4,64,512]{2,1,0:T(8,128)}) custom-call(f32[32,128]{1,0:T(8,128)S(1)} %bitcast.4, f32[4,64,512]{2,1,0:T(8,128)S(1)} %copy-done.5, f32[4,64,512]{2,1,0:T(8,128)S(1)} %copy-done.4, f32[4,64,512]{2,1,0:T(8,128)S(1)} %copy-done, f32[4,64,512]{2,1,0:T(8,128)S(1)} %get-tuple-element.16.img_ref), custom_call_target="tpu_custom_call" | custom-call | tf_op jit(solution)/shard_map/update/pallas_call | solution.py:334
  (2 shorter events, 0.0 us)
Async XLA Ops:
  0.6 7.1 %copy-start.4 = (f32[4,64,512]{2,1,0:T(8,128)S(1)}, f32[4,64,512]{2,1,0:T(8,128)}, u32[]{:S(2)}) copy-start(f32[4,64,512]{2,1,0:T(8,128)} %r_ref.5) | copy-start | bytes 1572868
  1.6 6.1 %copy-start = (f32[4,64,512]{2,1,0:T(8,128)S(1)}, f32[4,64,512]{2,1,0:T(8,128)}, u32[]{:S(2)}) copy-start(f32[4,64,512]{2,1,0:T(8,128)} %u_ref.5) | copy-start | bytes 1572868
  1.6 6.1 %copy-start.1 = (f32[4,64,512]{2,1,0:T(8,128)S(1)}, f32[4,64,512]{2,1,0:T(8,128)}, u32[]{:S(2)}) copy-start(f32[4,64,512]{2,1,0:T(8,128)} %w_ref.3) | copy-start | bytes 1572868
  1.7 6.1 %copy-start.2 = (f32[4,64,512]{2,1,0:T(8,128)S(1)}, f32[4,64,512]{2,1,0:T(8,128)}, u32[]{:S(2)}) copy-start(f32[4,64,512]{2,1,0:T(8,128)} %sil_ref.3) | copy-start | bytes 1572868
  1.7 6.1 %copy-start.3 = (f32[4,64,512]{2,1,0:T(8,128)S(1)}, f32[4,64,512]{2,1,0:T(8,128)}, u32[]{:S(2)}) copy-start(f32[4,64,512]{2,1,0:T(8,128)} %sxl_ref.3) | copy-start | bytes 1572868
  1.7 8.6 %collective-permute-start.1 = (f32[64,512]{1,0:T(8,128)S(1)}, f32[64,512]{1,0:T(8,128)S(1)}, u32[]{:S(2)}, u32[]{:S(2)}) collective-permute-start(f32[64,512]{1,0:T(8,128)S(1)} %pick.1._), channel_id=1, source_target_pairs={{0,1},{1,0},{2,4},{3,5},{4,2},{5,3},{6,8},{7,9},{8,6},{9,7},{10,12... | collective-permute-start | bytes 393224 | tf_op jit(solution)/shard_map/ppermute | solution.py:322
  6.0 4.3 %collective-permute-start = (f32[64,512]{1,0:T(8,128)S(1)}, f32[64,512]{1,0:T(8,128)S(1)}, u32[]{:S(2)}, u32[]{:S(2)}) collective-permute-start(f32[64,512]{1,0:T(8,128)S(1)} %get-tuple-element.13), channel_id=1, source_target_pairs={{0,2},{1,3},{2,0},{3,1},{4,6},{5,7},{6,4},{7,5},{8,10},{9,11},{10,... | collective-permute-start | bytes 393224 | tf_op jit(solution)/shard_map/ppermute | solution.py:328
  6.2 7.1 %collective-permute-start.2 = (f32[64,512]{1,0:T(8,128)S(1)}, f32[64,512]{1,0:T(8,128)S(1)}, u32[]{:S(2)}, u32[]{:S(2)}) collective-permute-start(f32[64,512]{1,0:T(8,128)S(1)} %get-tuple-element.12.mine_ref), channel_id=1, source_target_pairs={{0,2},{2,4},{4,6},{6,8},{8,10},{10,12},{12,14},{14,16},{16,18},{18... | collective-permute-start | bytes 393224 | tf_op jit(solution)/shard_map/ppermute | solution.py:324
  6.6 3.7 %collective-permute-start.3 = (f32[8,512]{1,0:T(8,128)S(1)}, f32[8,512]{1,0:T(8,128)S(1)}, u32[]{:S(2)}, u32[]{:S(2)}) collective-permute-start(f32[8,512]{1,0:T(8,128)S(1)} %get-tuple-element.14.rest_0_), channel_id=1, source_target_pairs={{0,1},{2,3},{4,5},{6,7},{8,9},{10,11},{12,13},{14,15},{16,17},{18,... | collective-permute-start | bytes 49160 | tf_op jit(solution)/shard_map/ppermute | solution.py:327
  13.3 10.6 %copy-start.5 = (f32[4,64,512]{2,1,0:T(8,128)S(1)}, f32[4,64,512]{2,1,0:T(8,128)}, u32[]{:S(2)}) copy-start(f32[4,64,512]{2,1,0:T(8,128)} %x_ref.1) | copy-start | bytes 1572868
where the time goes:
time: 25.4 us; the launch traced here: 25.3 us
  blocking collectives  10.1 us (40%)
  Pallas kernels  5.16 us (20%)
  starting transfers between devices  4.8 us (19%)
  waiting for transfers between devices  4.45 us (18%)
  between operations  0.71 us (3%)
    all_to_all x1, blocking collectives, step(): rows_all = lax.all_to_all(row, axes, 0, 0, tiled=True)  10.1 us
    ppermute x1, starting transfers between devices, step(): odd = lax.ppermute(picked, axes, odd_swap)  3.03 us
    ppermute x1, waiting for transfers between devices, step(): g_got = lax.ppermute(g, 'il', up)  2.98 us
    ppermute x1, waiting for transfers between devices, step(): xl_got.append(lax.ppermute(buf, axes, xl_swaps[p][0]))  1.47 us
    pallas_call x1, Pallas kernels, step(): return make_update(rows, cols, steps)(rows_all, x, r, u, image)  1.36 us
    pallas_call x1, Pallas kernels, step(): make_pack(rows, cols, steps, xl_parities)(picked, *stay)  1.27 us
    ppermute x1, starting transfers between devices, step(): xl_got.append(lax.ppermute(buf, axes, xl_swaps[p][0]))  1.2 us
    pallas_call x1, Pallas kernels, step(): part, sums = make_inner(rows, cols, steps)(u, r, s_il, s_xl, w)  1.05 us
  transfers between devices with their start and end apart: 4, of which 2 were waited for; matrix products, arithmetic and copies ran while one was open for 0% of the time, Pallas kernels for 9%

commit v1 on v0

v1 whole, which is shorter than its diff:
```python
import jax
import jax.numpy as jnp
from jax import lax
from jax.experimental import pallas as pl
from jax.experimental.pallas import tpu as pltpu
from jax.sharding import PartitionSpec as P


damping = 0.3
VMEM_LIMIT = 16 * 1024 * 1024


def swap_pairs(sizes, axis, parity):
    n_il, n_xl = sizes
    size, other = (n_il, n_xl) if axis == 0 else (n_xl, n_il)
    pairs, real = [], False
    for a in range(size):
        mate = a + 1 if a % 2 == parity else a - 1
        inside = 0 <= mate < size
        real = real or inside
        for b in range(other):
            if inside:
                a_to, b_to = mate, b
            else:
                a_to, b_to = a, (b ^ 1 if (b ^ 1) < other else b)
            here, there = ((a, b), (a_to, b_to)) if axis == 0 else ((b, a), (b_to, a_to))
            pairs.append((here[0] * n_xl + here[1], there[0] * n_xl + there[1]))
    return pairs, real


def time_diff(field):
    steps = field.shape[-1]
    at = lax.broadcasted_iota(jnp.int32, field.shape, field.ndim - 1)
    after = jnp.where(at == steps - 1, 0.0, pltpu.roll(field, steps - 1, field.ndim - 1))
    before = jnp.where(at == 0, 0.0, pltpu.roll(field, 1, field.ndim - 1))
    return 0.5 * (after - before)


def params():
    return pltpu.CompilerParams(vmem_limit_bytes=VMEM_LIMIT)


VMEM = pl.BlockSpec(memory_space=pltpu.VMEM)
HBM = pl.BlockSpec(memory_space=pltpu.HBM)


def f32(*shape):
    return jax.ShapeDtypeStruct(shape, jnp.float32)


def make_slope_row(rows, cols, steps):
    def kernel(u_hbm, sil_hbm, g_ref, u_ref, s_ref, sems):
        @pl.when(lax.axis_index("il") % 2 == 1)
        def _():
            pairs = ((u_hbm.at[rows - 1], u_ref), (sil_hbm.at[rows - 1], s_ref))
            copies = [pltpu.make_async_copy(src, dst, sems.at[k]) for k, (src, dst) in enumerate(pairs)]
            for copy in copies:
                copy.start()
            for copy in copies:
                copy.wait()
            u = u_ref[...]
            g_ref[...] = u + s_ref[...] * time_diff(u)

    return pl.pallas_call(
        kernel,
        in_specs=[HBM] * 2,
        out_specs=VMEM,
        out_shape=f32(cols, steps),
        scratch_shapes=[pltpu.VMEM((cols, steps), jnp.float32)] * 2 + [pltpu.SemaphoreType.DMA((2,))],
        compiler_params=params(),
        name="slope_row",
    )


def make_pick(rows, cols, steps):
    def kernel(_, u_ref, w_ref, odd_ref):
        il_odd = lax.axis_index("il") % 2

        @pl.when(il_odd == 0)
        def _():
            odd_ref[...] = u_ref[0]

        @pl.when(il_odd == 1)
        def _():
            odd_ref[...] = w_ref[rows - 1]

    return pl.pallas_call(
        kernel,
        in_specs=[pl.BlockSpec(memory_space=pl.ANY), VMEM, VMEM],
        out_specs=VMEM,
        out_shape=f32(cols, steps),
        compiler_params=params(),
        name="pick",
    )


def make_pack(rows, cols, steps, xl_parities):
    edge = min(8, cols)

    def kernel(_, u_hbm, sil_hbm, sxl_hbm, w_hbm, even_ref, *rest):
        bufs = rest[: len(xl_parities)]
        u_low, s_low, u_cl, s_cl, w_cl, u_cu, sems = rest[len(xl_parities) :]
        il_odd = lax.axis_index("il") % 2
        xl_odd = lax.axis_index("xl") % 2
        last, first = pl.ds(cols - edge, edge), pl.ds(0, edge)
        pairs = (
            (u_hbm.at[:, last], u_cl),
            (sxl_hbm.at[:, last], s_cl),
            (w_hbm.at[:, last], w_cl),
            (u_hbm.at[:, first], u_cu),
        )
        copies = [pltpu.make_async_copy(src, dst, sems.at[k]) for k, (src, dst) in enumerate(pairs)]
        for copy in copies:
            copy.start()

        @pl.when(il_odd == 0)
        def _():
            pairs = ((u_hbm.at[rows - 1], u_low), (sil_hbm.at[rows - 1], s_low), (w_hbm.at[rows - 1], even_ref.at[0]))
            low = [pltpu.make_async_copy(src, dst, sems.at[4 + k]) for k, (src, dst) in enumerate(pairs)]
            for copy in low:
                copy.start()
            for copy in low:
                copy.wait()
            u = u_low[...]
            even_ref[1] = u + s_low[...] * time_diff(u)

        @pl.when(il_odd == 1)
        def _():
            copy = pltpu.make_async_copy(u_hbm.at[0], even_ref.at[0], sems.at[4])
            copy.start()
            copy.wait()

        for copy in copies:
            copy.wait()
        u = u_cl[:, edge - 1, :]
        g = u + s_cl[:, edge - 1, :] * time_diff(u)
        for parity, buf in zip(xl_parities, bufs):
            buf[pl.ds(rows, rows)] = g

            @pl.when(xl_odd == parity)
            def _(buf=buf):
                buf[pl.ds(0, rows)] = w_cl[:, edge - 1, :]

            @pl.when(xl_odd != parity)
            def _(buf=buf):
                buf[pl.ds(0, rows)] = u_cu[:, 0, :]

    outs = [f32(2, cols, steps)] + [f32(2 * rows, steps)] * len(xl_parities)
    return pl.pallas_call(
        kernel,
        in_specs=[pl.BlockSpec(memory_space=pl.ANY)] + [HBM] * 4,
        out_specs=[VMEM] * len(outs),
        out_shape=outs,
        scratch_shapes=[pltpu.VMEM((cols, steps), jnp.float32)] * 2
        + [pltpu.VMEM((rows, edge, steps), jnp.float32)] * 4
        + [pltpu.SemaphoreType.DMA((7,))],
        compiler_params=params(),
        name="pack",
    )


def edge_tiles(cols):
    return sorted({0, cols - 8})


def inner_tiles(cols):
    return range(8, cols - 8, 8)


def add_products(sums, tiles, u_ref, r_ref, img_ref):
    for i, j in tiles:
        at = (i, pl.ds(j, 8))
        u, r, image = u_ref[at], r_ref[at], img_ref[at]
        sums = [s + a * b for s, (a, b) in zip(sums, ((u, image), (r, image), (image, image)))]
    return sums


def lower_flux(w, ahead, g, slope):
    flux = w * w * (ahead - g)
    return time_diff(slope * flux) - flux


def make_inner(rows, cols, steps):
    def kernel(u_ref, r_ref, sil_ref, sxl_ref, w_ref, img_ref, sums_ref):
        col = lax.broadcasted_iota(jnp.int32, (cols, steps), 0)
        flux_before = None
        norm = jnp.zeros((8, steps), jnp.float32)
        sums = [norm] * 3
        for i in range(rows):
            u = u_ref[i]
            w2 = w_ref[i] * w_ref[i]
            slope_t = time_diff(u)
            s_xl = sxl_ref[i]
            ahead = pltpu.roll(u, cols - 1, 0)
            flux_xl = jnp.where(col == cols - 1, 0.0, w2 * (ahead - u - s_xl * slope_t))
            behind = jnp.where(col == 0, 0.0, pltpu.roll(flux_xl, 1, 0))
            image = behind - flux_xl + damping * u
            along = s_xl * flux_xl
            if flux_before is not None:
                image = image + flux_before
            if i < rows - 1:
                s_il = sil_ref[i]
                flux_il = w2 * (u_ref[i + 1] - u - s_il * slope_t)
                image = image - flux_il
                along = along + s_il * flux_il
                flux_before = flux_il
            img_ref[i] = image + time_diff(along)
            for j in range(0, cols, 8):
                r = r_ref[i, pl.ds(j, 8)]
                norm = norm + r * r
            if 0 < i < rows - 1:
                sums = add_products(sums, [(i, j) for j in inner_tiles(cols)], u_ref, r_ref, img_ref)
        for k, value in enumerate([norm] + sums):
            sums_ref[k] = value

    return pl.pallas_call(
        kernel,
        in_specs=[VMEM] * 5,
        out_specs=[VMEM] * 2,
        out_shape=[f32(rows, cols, steps), f32(4, 8, steps)],
        compiler_params=params(),
        name="inner",
    )


def make_even_edge(rows, cols, steps, n_il):
    def kernel(u_ref, r_ref, sil_ref, w_ref, mine_ref, got_ref, _, img_in, sums_in, img_ref, sums_ref):
        il = lax.axis_index("il")

        def add(row):
            if rows > 1:
                sums = add_products(
                    [sums_ref[k] for k in range(1, 4)], [(row, j) for j in inner_tiles(cols)], u_ref, r_ref, img_ref
                )
                for k, value in enumerate(sums):
                    sums_ref[k + 1] = value

        @pl.when(il % 2 == 0)
        def _():
            @pl.when(il < n_il - 1)
            def _():
                img_ref[rows - 1] += lower_flux(w_ref[rows - 1], got_ref[0], mine_ref[1], sil_ref[rows - 1])

            add(rows - 1)

        @pl.when(il % 2 == 1)
        def _():
            img_ref[0] += got_ref[0] * got_ref[0] * (u_ref[0] - got_ref[1])
            add(0)

    return pl.pallas_call(
        kernel,
        in_specs=[VMEM] * 6 + [pl.BlockSpec(memory_space=pl.ANY)] + [VMEM] * 2,
        out_specs=[VMEM] * 2,
        out_shape=[f32(rows, cols, steps), f32(4, 8, steps)],
        input_output_aliases={7: 0, 8: 1},
        compiler_params=params(),
        name="even_edge",
    )


def make_edges(rows, cols, steps, n_il, n_xl, xl_parities, n_dev):
    def kernel(u_ref, r_ref, sil_ref, sxl_ref, w_ref, part_ref, sums_in, own_ref, odd_ref, g_ref, *rest):
        bufs = rest[:-3]
        img_ref, out_ref, sums_ref = rest[-3:]
        il, xl = lax.axis_index("il"), lax.axis_index("xl")

        half = len(xl_parities)
        for parity, mine, got in zip(xl_parities, bufs[:half], bufs[half:]):

            @pl.when((xl % 2 == parity) & (xl < n_xl - 1))
            def _(mine=mine, got=got):
                here, there = pl.ds(0, rows), pl.ds(rows, rows)
                add = lower_flux(mine[here], got[here], mine[there], sxl_ref[:, cols - 1, :])
                for i in range(rows):
                    img_ref[i, pl.ds(cols - 1, 1), :] += add[i : i + 1]

            @pl.when((xl % 2 != parity) & (xl > 0))
            def _(got=got):
                w = got[pl.ds(0, rows)]
                add = w * w * (u_ref[:, 0, :] - got[pl.ds(rows, rows)])
                for i in range(rows):
                    img_ref[i, pl.ds(0, 1), :] += add[i : i + 1]

        def add(row):
            tiles = [(row, j) for j in inner_tiles(cols)]
            tiles += [(i, j) for i in range(rows) for j in edge_tiles(cols)]
            sums = add_products([sums_in[k] for k in range(1, 4)], tiles, u_ref, r_ref, img_ref)
            for k, value in enumerate(sums):
                sums_ref[k] = value

        @pl.when(il % 2 == 0)
        def _():
            @pl.when(il > 0)
            def _():
                w = odd_ref[...]
                img_ref[0] += w * w * (u_ref[0] - g_ref[...])

            add(0)

        @pl.when(il % 2 == 1)
        def _():
            @pl.when(il < n_il - 1)
            def _():
                img_ref[rows - 1] += lower_flux(w_ref[rows - 1], odd_ref[...], own_ref[...], sil_ref[rows - 1])

            add(rows - 1)

        lane = lax.broadcasted_iota(jnp.int32, (1, 128), 1)
        row = jnp.zeros((1, 128), jnp.float32)
        for k, value in enumerate([sums_in[0]] + [sums_ref[k] for k in range(3)]):
            value = sum(value[:, j : j + 128] for j in range(128, steps, 128)) + value[:, :128]
            value = jnp.sum(jnp.sum(value, axis=0, keepdims=True), axis=1, keepdims=True)
            row = jnp.where(lane == k, value, row)
        out_ref[...] = jnp.broadcast_to(row, (n_dev, 128))

    return pl.pallas_call(
        kernel,
        in_specs=[VMEM] * (10 + 2 * len(xl_parities)),
        out_specs=[VMEM, VMEM],
        out_shape=[f32(rows, cols, steps), f32(n_dev, 128)],
        input_output_aliases={5: 0},
        scratch_shapes=[pltpu.VMEM((3, 8, steps), jnp.float32)],
        compiler_params=params(),
        name="edges",
    )


def make_update(rows, cols, steps):
    piece = 64 if cols % 64 == 0 else cols

    def kernel(sums_ref, x_ref, r_ref, u_ref, img_ref, x_hbm, r_hbm, d_hbm, x_out, r_out, d_out, sems):
        total = jnp.sum(sums_ref[...], axis=0, keepdims=True)
        lane = lax.broadcasted_iota(jnp.int32, total.shape, 1)
        norm_old, along, cross, square = (
            jnp.sum(jnp.where(lane == k, total, 0.0), axis=1, keepdims=True) for k in range(4)
        )
        alpha = norm_old / along
        norm_new = norm_old - 2.0 * alpha * cross + alpha * alpha * square
        beta = norm_new / norm_old
        copies = []
        pieces = [(i, pl.ds(j, piece)) for i in range(rows) for j in range(0, cols, piece)]
        for n, at in enumerate(pieces):
            u = u_ref[at]
            residual = r_ref[at] - alpha * img_ref[at]
            x_out[at] = x_ref[at] + alpha * u
            r_out[at] = residual
            d_out[at] = residual + beta * u
            for k, (src, dst) in enumerate(((x_out, x_hbm), (r_out, r_hbm), (d_out, d_hbm))):
                copy = pltpu.make_async_copy(src.at[at], dst.at[at], sems.at[k, n])
                copy.start()
                copies.append(copy)
        for copy in copies:
            copy.wait()

    return pl.pallas_call(
        kernel,
        in_specs=[VMEM] * 5,
        out_specs=[HBM] * 3,
        out_shape=[f32(rows, cols, steps)] * 3,
        scratch_shapes=[pltpu.VMEM((rows, cols, steps), jnp.float32)] * 3
        + [pltpu.SemaphoreType.DMA((3, rows * cols // piece))],
        compiler_params=params(),
        name="update",
    )


def solution(mesh):
    n_il, n_xl = mesh.shape["il"], mesh.shape["xl"]
    n_dev = n_il * n_xl
    axes = ("il", "xl")
    even_swap, odd_swap = (swap_pairs((n_il, n_xl), 0, parity)[0] for parity in range(2))
    up = [(i, (i + 1) % n_il) for i in range(n_il)]
    xl_swaps = [swap_pairs((n_il, n_xl), 1, parity) for parity in range(2)]
    xl_parities = [parity for parity in range(2) if xl_swaps[parity][1]]

    def step(x, r, u, s_il, s_xl, w):
        rows, cols, steps = u.shape
        stay = [pltpu.with_memory_space_constraint(a, pltpu.HBM) for a in (u, s_il, s_xl, w)]
        g = make_slope_row(rows, cols, steps)(stay[0], stay[1])
        g_got = lax.ppermute(g, "il", up)
        odd_sent = make_pick(rows, cols, steps)(g, u, w)
        odd = lax.ppermute(odd_sent, axes, odd_swap)
        even_sent, *xl_sent = make_pack(rows, cols, steps, xl_parities)(odd_sent, *stay)
        xl_got = []
        for p, buf in zip(xl_parities, xl_sent):
            xl_got.append(lax.ppermute(buf, axes, xl_swaps[p][0]))
        even = lax.ppermute(even_sent, axes, even_swap)
        part, sums = make_inner(rows, cols, steps)(u, r, s_il, s_xl, w)
        part, sums = make_even_edge(rows, cols, steps, n_il)(u, r, s_il, w, even_sent, even, even_sent, part, sums)
        image, row = make_edges(rows, cols, steps, n_il, n_xl, xl_parities, n_dev)(
            u, r, s_il, s_xl, w, part, sums, g, odd, g_got, *xl_sent, *xl_got
        )
        rows_all = lax.all_to_all(row, axes, 0, 0, tiled=True)
        return make_update(rows, cols, steps)(rows_all, x, r, u, image)

    placed = P("il", "xl", None)
    return jax.shard_map(step, mesh=mesh, in_specs=(placed,) * 6, out_specs=(placed,) * 3, check_vma=False)
```

time: 25.4 us -> 26.2 us (1.031)
  local copies, waits for them, and re-layouts: 0.03 us -> 1.18 us
  Pallas kernels: 5.16 us -> 4.52 us
  blocking collectives: 10.1 us -> 10.7 us
  waiting for transfers between devices: 4.45 us -> 4.16 us
    unnamed x12 -> x16, local copies, waits for them, and re-layouts: 0.03 us -> 1.18 us
    all_to_all x1, blocking collectives: 10.1 us -> 10.7 us  [step(): rows_all = lax.all_to_all(row, axes, 0, 0, tiled=True)]
    ppermute x1, waiting for transfers between devices: 1.47 us -> 0.95 us  [step(): xl_got.append(lax.ppermute(buf, axes, xl_swaps[p][0]))]
    pallas_call x2 -> x4, Pallas kernels: 2.25 us -> 1.86 us  [the longest x1 1.61 us: step(): make_pack(rows, cols, steps, xl_parities)(odd_sent, *stay)]
    ppermute x1, starting transfers between devices: 1.2 us -> 1.5 us  [step(): xl_got.append(lax.ppermute(buf, axes, xl_swaps[p][0]))]
  transfers between devices with their start and end apart: 4 -> 4, of which waited for: 2 -> 2; matrix products, arithmetic and copies ran while one was open for 0% -> 0% of each run, Pallas kernels for 9% -> 5%
where the time goes in v1:
time: 26.2 us; the launch traced here: 26 us
  blocking collectives  10.7 us (41%)
  starting transfers between devices  4.75 us (18%)
  Pallas kernels  4.52 us (17%)
  waiting for transfers between devices  4.16 us (16%)
  local copies, waits for them, and re-layouts  1.18 us (5%)
  between operations  0.74 us (3%)
    all_to_all x1, blocking collectives, step(): rows_all = lax.all_to_all(row, axes, 0, 0, tiled=True)  10.7 us
    ppermute x1, waiting for transfers between devices, step(): g_got = lax.ppermute(g, 'il', up)  3.21 us
    ppermute x1, starting transfers between devices, step(): odd = lax.ppermute(odd_sent, axes, odd_swap)  2.7 us
    pallas_call x1, Pallas kernels, step(): make_pack(rows, cols, steps, xl_parities)(odd_sent, *stay)  1.61 us
    ppermute x1, starting transfers between devices, step(): xl_got.append(lax.ppermute(buf, axes, xl_swaps[p][0]))  1.5 us
    pallas_call x1, Pallas kernels, step(): return make_update(rows, cols, steps)(rows_all, x, r, u, image)  1.36 us
    unnamed x16, local copies, waits for them, and re-layouts  1.18 us
    pallas_call x1, Pallas kernels, step(): part, sums = make_inner(rows, cols, steps)(u, r, s_il, s_xl, w)  1.05 us
  transfers between devices with their start and end apart: 4, of which 2 were waited for; matrix products, arithmetic and copies ran while one was open for 0% of the time, Pallas kernels for 5%

profile of v1, /device:TPU:0, one launch (start us, length us, event | category | flops | bytes accessed | tf_op | source)
XLA Modules:
  0.0 26.0 jit_solution(7314736939610098156)
XLA Ops:
  0.6 0.0 copy-start
  0.6 0.0 copy-start.3
  0.7 1.0 %copy-done = f32[4,64,512]{2,1,0:T(8,128)S(1)} copy-done((f32[4,64,512]{2,1,0:T(8,128)S(1)}, f32[4,64,512]{2,1,0:T(8,128)}, u32[]{:S(2)}) %copy-start) | copy-done | bytes 524312
  1.7 0.2 copy-done.3
  1.9 0.0 copy-start.1
  1.9 0.0 copy-start.2
  1.9 0.0 copy-start.4
  1.9 0.0 copy-start.5
  1.9 1.6 %pack.1 = (f32[2,64,512]{2,1,0:T(8,128)S(1)}, f32[8,512]{1,0:T(8,128)S(1)}) custom-call(f32[64,512]{1,0:T(8,128)S(1)} %pick.1._, f32[4,64,512]{2,1,0:T(8,128)} %u_ref.9, f32[4,64,512]{2,1,0:T(8,128)} %sil_ref.5, f32[4,64,512]{2,1,0:T(8,128)} %sxl_ref.3, f32[4,64,512]{2,1,0:T(8,128)} %w_ref.7), custom_call_target="tpu_custom_call" | custom-call | tf_op jit(solution)/shard_map/pack/pallas_call | solution.py:384
  3.5 0.4 %collective-permute-start = (f32[2,64,512]{2,1,0:T(8,128)S(1)}, f32[2,64,512]{2,1,0:T(8,128)S(1)}, u32[]{:S(2)}, u32[]{:S(2)}) collective-permute-start(f32[2,64,512]{2,1,0:T(8,128)S(1)} %get-tuple-element.11.mine_ref._), channel_id=1, source_target_pairs={{0,2},{1,3},{2,0},{3,1},{4,6},{5,7},{6,4},{7,5},{8,10},{9,11},{10,... | collective-permute-start | bytes 786440 | tf_op jit(solution)/shard_map/ppermute | solution.py:388
  3.9 2.7 %collective-permute-start.1 = (f32[64,512]{1,0:T(8,128)S(1)}, f32[64,512]{1,0:T(8,128)S(1)}, u32[]{:S(2)}, u32[]{:S(2)}) collective-permute-start(f32[64,512]{1,0:T(8,128)S(1)} %pick.1._), channel_id=1, source_target_pairs={{0,1},{1,0},{2,4},{3,5},{4,2},{5,3},{6,8},{7,9},{8,6},{9,7},{10,12... | collective-permute-start | bytes 393224 | tf_op jit(solution)/shard_map/ppermute | solution.py:383
  6.6 0.1 collective-permute-start.2
  6.8 1.5 %collective-permute-start.3 = (f32[8,512]{1,0:T(8,128)S(1)}, f32[8,512]{1,0:T(8,128)S(1)}, u32[]{:S(2)}, u32[]{:S(2)}) collective-permute-start(f32[8,512]{1,0:T(8,128)S(1)} %get-tuple-element.16.rest_0_), channel_id=1, source_target_pairs={{0,1},{2,3},{4,5},{6,7},{8,9},{10,11},{12,13},{14,15},{16,17},{18,... | collective-permute-start | bytes 49160 | tf_op jit(solution)/shard_map/ppermute | solution.py:387
  8.3 0.0 copy-done.6
  8.3 0.0 copy-done.5
  8.3 1.0 %inner.1 = (f32[4,64,512]{2,1,0:T(8,128)S(1)}, f32[4,8,512]{2,1,0:T(8,128)S(1)}) custom-call(f32[4,64,512]{2,1,0:T(8,128)S(1)} %copy-done.1, f32[4,64,512]{2,1,0:T(8,128)S(1)} %copy-done.5, f32[4,64,512]{2,1,0:T(8,128)S(1)} %copy-done.2, f32[4,64,512]{2,1,0:T(8,128)S(1)} %copy-done.6, f32[4,64,512]{2,1,0:T(8,128)S(1)} %copy-done.4), custom_call_target="tpu_custom_call" | custom-call | tf_op jit(solution)/shard_map/inner/pallas_call | solution.py:389
  9.3 0.0 collective-permute-done.got_ref
  9.4 0.2 even_edge.1
  9.6 0.9 %collective-permute-done.3.rest_1_ = f32[8,512]{1,0:T(8,128)S(1)} collective-permute-done((f32[8,512]{1,0:T(8,128)S(1)}, f32[8,512]{1,0:T(8,128)S(1)}, u32[]{:S(2)}, u32[]{:S(2)}) %collective-permute-start.3) | collective-permute-done | bytes 16416 | tf_op jit(solution)/shard_map/ppermute | solution.py:387
  10.5 0.0 collective-permute-done.1.odd_ref
  10.5 3.2 %collective-permute-done.2.g_ref = f32[64,512]{1,0:T(8,128)S(1)} collective-permute-done((f32[64,512]{1,0:T(8,128)S(1)}, f32[64,512]{1,0:T(8,128)S(1)}, u32[]{:S(2)}, u32[]{:S(2)}) %collective-permute-start.2) | collective-permute-done | bytes 131104 | tf_op jit(solution)/shard_map/ppermute | solution.py:381
  13.7 0.3 edges.1
  14.0 10.7 %all_to_all.11 = f32[32,1,128]{2,1,0:T(1,128)S(1)} all-to-all(f32[32,1,128]{2,1,0:T(1,128)S(1)} %bitcast.5), channel_id=1, replica_groups=mesh['il'=16,'xl'=2] {'il','xl'}, dimensions={0} | all-to-all | bytes 32768 | tf_op jit(solution)/shard_map/all_to_all | solution.py:394
  24.6 1.4 %update.1 = (f32[4,64,512]{2,1,0:T(8,128)}, f32[4,64,512]{2,1,0:T(8,128)}, f32[4,64,512]{2,1,0:T(8,128)}) custom-call(f32[32,128]{1,0:T(8,128)S(1)} %bitcast.4, f32[4,64,512]{2,1,0:T(8,128)S(1)} %copy-done.7, f32[4,64,512]{2,1,0:T(8,128)S(1)} %copy-done.5, f32[4,64,512]{2,1,0:T(8,128)S(1)} %copy-done.1, f32[4,64,512]{2,1,0:T(8,128)S(1)} %get-tuple-element.18.img_ref), custom_call_target="tpu_custom_call" | custom-call | tf_op jit(solution)/shard_map/update/pallas_call | solution.py:395
  (8 shorter events, 0.1 us)
Async XLA Ops:
  0.6 1.0 %copy-start = (f32[4,64,512]{2,1,0:T(8,128)S(1)}, f32[4,64,512]{2,1,0:T(8,128)}, u32[]{:S(2)}) copy-start(f32[4,64,512]{2,1,0:T(8,128)} %u_ref.9) | copy-start | bytes 1572868
  0.6 1.2 %copy-start.3 = (f32[4,64,512]{2,1,0:T(8,128)S(1)}, f32[4,64,512]{2,1,0:T(8,128)}, u32[]{:S(2)}) copy-start(f32[4,64,512]{2,1,0:T(8,128)} %w_ref.7) | copy-start | bytes 1572868
  1.8 6.4 %copy-start.6 = (f32[4,64,512]{2,1,0:T(8,128)S(1)}, f32[4,64,512]{2,1,0:T(8,128)}, u32[]{:S(2)}) copy-start(f32[4,64,512]{2,1,0:T(8,128)} %sxl_ref.3) | copy-start | bytes 1572868
  1.9 6.4 %copy-start.1 = (f32[4,64,512]{2,1,0:T(8,128)S(1)}, f32[4,64,512]{2,1,0:T(8,128)}, u32[]{:S(2)}) copy-start(f32[4,64,512]{2,1,0:T(8,128)} %u_ref.9) | copy-start | bytes 1572868
  1.9 6.4 %copy-start.2 = (f32[4,64,512]{2,1,0:T(8,128)S(1)}, f32[4,64,512]{2,1,0:T(8,128)}, u32[]{:S(2)}) copy-start(f32[4,64,512]{2,1,0:T(8,128)} %sil_ref.5) | copy-start | bytes 1572868
  1.9 6.4 %copy-start.4 = (f32[4,64,512]{2,1,0:T(8,128)S(1)}, f32[4,64,512]{2,1,0:T(8,128)}, u32[]{:S(2)}) copy-start(f32[4,64,512]{2,1,0:T(8,128)} %w_ref.7) | copy-start | bytes 1572868
  1.9 6.4 %copy-start.5 = (f32[4,64,512]{2,1,0:T(8,128)S(1)}, f32[4,64,512]{2,1,0:T(8,128)}, u32[]{:S(2)}) copy-start(f32[4,64,512]{2,1,0:T(8,128)} %r_ref.7) | copy-start | bytes 1572868
  3.5 5.8 %collective-permute-start = (f32[2,64,512]{2,1,0:T(8,128)S(1)}, f32[2,64,512]{2,1,0:T(8,128)S(1)}, u32[]{:S(2)}, u32[]{:S(2)}) collective-permute-start(f32[2,64,512]{2,1,0:T(8,128)S(1)} %get-tuple-element.11.mine_ref._), channel_id=1, source_target_pairs={{0,2},{1,3},{2,0},{3,1},{4,6},{5,7},{6,4},{7,5},{8,10},{9,11},{10,... | collective-permute-start | bytes 786440 | tf_op jit(solution)/shard_map/ppermute | solution.py:388
  3.9 6.6 %collective-permute-start.1 = (f32[64,512]{1,0:T(8,128)S(1)}, f32[64,512]{1,0:T(8,128)S(1)}, u32[]{:S(2)}, u32[]{:S(2)}) collective-permute-start(f32[64,512]{1,0:T(8,128)S(1)} %pick.1._), channel_id=1, source_target_pairs={{0,1},{1,0},{2,4},{3,5},{4,2},{5,3},{6,8},{7,9},{8,6},{9,7},{10,12... | collective-permute-start | bytes 393224 | tf_op jit(solution)/shard_map/ppermute | solution.py:383
  6.6 7.1 %collective-permute-start.2 = (f32[64,512]{1,0:T(8,128)S(1)}, f32[64,512]{1,0:T(8,128)S(1)}, u32[]{:S(2)}, u32[]{:S(2)}) collective-permute-start(f32[64,512]{1,0:T(8,128)S(1)} %slope_row.1._.own_ref), channel_id=1, source_target_pairs={{0,2},{2,4},{4,6},{6,8},{8,10},{10,12},{12,14},{14,16},{16,18},{18... | collective-permute-start | bytes 393224 | tf_op jit(solution)/shard_map/ppermute | solution.py:381
  6.8 3.7 %collective-permute-start.3 = (f32[8,512]{1,0:T(8,128)S(1)}, f32[8,512]{1,0:T(8,128)S(1)}, u32[]{:S(2)}, u32[]{:S(2)}) collective-permute-start(f32[8,512]{1,0:T(8,128)S(1)} %get-tuple-element.16.rest_0_), channel_id=1, source_target_pairs={{0,1},{2,3},{4,5},{6,7},{8,9},{10,11},{12,13},{14,15},{16,17},{18,... | collective-permute-start | bytes 49160 | tf_op jit(solution)/shard_map/ppermute | solution.py:387
  13.7 10.9 %copy-start.7 = (f32[4,64,512]{2,1,0:T(8,128)S(1)}, f32[4,64,512]{2,1,0:T(8,128)}, u32[]{:S(2)}) copy-start(f32[4,64,512]{2,1,0:T(8,128)} %x_ref.1) | copy-start | bytes 1572868

commit v2 on v1

--- a/solution.py
+++ b/solution.py
@@ -95,67 +95,52 @@
 
 
 def make_pack(rows, cols, steps, xl_parities):
-    edge = min(8, cols)
-
-    def kernel(_, u_hbm, sil_hbm, sxl_hbm, w_hbm, even_ref, *rest):
-        bufs = rest[: len(xl_parities)]
-        u_low, s_low, u_cl, s_cl, w_cl, u_cu, sems = rest[len(xl_parities) :]
-        il_odd = lax.axis_index("il") % 2
+    def kernel(_, u_ref, sxl_ref, w_ref, *bufs):
         xl_odd = lax.axis_index("xl") % 2
-        last, first = pl.ds(cols - edge, edge), pl.ds(0, edge)
-        pairs = (
-            (u_hbm.at[:, last], u_cl),
-            (sxl_hbm.at[:, last], s_cl),
-            (w_hbm.at[:, last], w_cl),
-            (u_hbm.at[:, first], u_cu),
-        )
-        copies = [pltpu.make_async_copy(src, dst, sems.at[k]) for k, (src, dst) in enumerate(pairs)]
-        for copy in copies:
-            copy.start()
-
-        @pl.when(il_odd == 0)
-        def _():
-            pairs = ((u_hbm.at[rows - 1], u_low), (sil_hbm.at[rows - 1], s_low), (w_hbm.at[rows - 1], even_ref.at[0]))
-            low = [pltpu.make_async_copy(src, dst, sems.at[4 + k]) for k, (src, dst) in enumerate(pairs)]
-            for copy in low:
-                copy.start()
-            for copy in low:
-                copy.wait()
-            u = u_low[...]
-            even_ref[1] = u + s_low[...] * time_diff(u)
-
-        @pl.when(il_odd == 1)
-        def _():
-            copy = pltpu.make_async_copy(u_hbm.at[0], even_ref.at[0], sems.at[4])
-            copy.start()
-            copy.wait()
-
-        for copy in copies:
-            copy.wait()
-        u = u_cl[:, edge - 1, :]
-        g = u + s_cl[:, edge - 1, :] * time_diff(u)
+        u = u_ref[:, cols - 1, :]
+        g = u + sxl_ref[:, cols - 1, :] * time_diff(u)
         for parity, buf in zip(xl_parities, bufs):
             buf[pl.ds(rows, rows)] = g
 
             @pl.when(xl_odd == parity)
             def _(buf=buf):
-                buf[pl.ds(0, rows)] = w_cl[:, edge - 1, :]
+                buf[pl.ds(0, rows)] = w_ref[:, cols - 1, :]
 
             @pl.when(xl_odd != parity)
             def _(buf=buf):
-                buf[pl.ds(0, rows)] = u_cu[:, 0, :]
-
-    outs = [f32(2, cols, steps)] + [f32(2 * rows, steps)] * len(xl_parities)
-    return pl.pallas_call(
-        kernel,
-        in_specs=[pl.BlockSpec(memory_space=pl.ANY)] + [HBM] * 4,
-        out_specs=[VMEM] * len(outs),
-        out_shape=outs,
-        scratch_shapes=[pltpu.VMEM((cols, steps), jnp.float32)] * 2
-        + [pltpu.VMEM((rows, edge, steps), jnp.float32)] * 4
-        + [pltpu.SemaphoreType.DMA((7,))],
+                buf[pl.ds(0, rows)] = u_ref[:, 0, :]
+
+    return pl.pallas_call(
+        kernel,
+        in_specs=[pl.BlockSpec(memory_space=pl.ANY)] + [VMEM] * 3,
+        out_specs=[VMEM] * len(xl_parities),
+        out_shape=[f32(2 * rows, steps)] * len(xl_parities),
         compiler_params=params(),
         name="pack",
+    )
+
+
+def make_pair(rows, cols, steps):
+    def kernel(_, u_ref, sil_ref, w_ref, even_ref):
+        il_odd = lax.axis_index("il") % 2
+
+        @pl.when(il_odd == 0)
+        def _():
+            u = u_ref[rows - 1]
+            even_ref[0] = w_ref[rows - 1]
+            even_ref[1] = u + sil_ref[rows - 1] * time_diff(u)
+
+        @pl.when(il_odd == 1)
+        def _():
+            even_ref[0] = u_ref[0]
+
+    return pl.pallas_call(
+        kernel,
+        in_specs=[pl.BlockSpec(memory_space=pl.ANY)] + [VMEM] * 3,
+        out_specs=VMEM,
+        out_shape=f32(2, cols, steps),
+        compiler_params=params(),
+        name="pair",
     )
 
 
@@ -376,15 +361,16 @@
 
     def step(x, r, u, s_il, s_xl, w):
         rows, cols, steps = u.shape
-        stay = [pltpu.with_memory_space_constraint(a, pltpu.HBM) for a in (u, s_il, s_xl, w)]
+        stay = [pltpu.with_memory_space_constraint(a, pltpu.HBM) for a in (u, s_il)]
         g = make_slope_row(rows, cols, steps)(stay[0], stay[1])
         g_got = lax.ppermute(g, "il", up)
         odd_sent = make_pick(rows, cols, steps)(g, u, w)
         odd = lax.ppermute(odd_sent, axes, odd_swap)
-        even_sent, *xl_sent = make_pack(rows, cols, steps, xl_parities)(odd_sent, *stay)
+        xl_sent = make_pack(rows, cols, steps, xl_parities)(odd_sent, u, s_xl, w)
         xl_got = []
         for p, buf in zip(xl_parities, xl_sent):
             xl_got.append(lax.ppermute(buf, axes, xl_swaps[p][0]))
+        even_sent = make_pair(rows, cols, steps)(xl_sent[0] if xl_sent else odd_sent, u, s_il, w)
         even = lax.ppermute(even_sent, axes, even_swap)
         part, sums = make_inner(rows, cols, steps)(u, r, s_il, s_xl, w)
         part, sums = make_even_edge(rows, cols, steps, n_il)(u, r, s_il, w, even_sent, even, even_sent, part, sums)

time: 26.2 us -> 26.8 us (1.023)
  local copies, waits for them, and re-layouts: 1.18 us -> 3.11 us
  Pallas kernels: 4.52 us -> 3.14 us
    unnamed x16 -> x12, local copies, waits for them, and re-layouts: 1.18 us -> 3.11 us
    pallas_call x1 -> x2, Pallas kernels: 1.61 us -> 0.23 us  [the longest x1 0.14 us: step(): make_pair(rows, cols, steps)]
where the time goes in v2:
time: 26.8 us; the launch traced here: 26.5 us
  blocking collectives  10.7 us (40%)
  starting transfers between devices  4.74 us (18%)
  waiting for transfers between devices  4.18 us (16%)
  Pallas kernels  3.14 us (12%)
  local copies, waits for them, and re-layouts  3.11 us (12%)
  between operations  0.71 us (3%)
    all_to_all x1, blocking collectives, step(): rows_all = lax.all_to_all(row, axes, 0, 0, tiled=True)  10.7 us
    ppermute x1, waiting for transfers between devices, step(): g_got = lax.ppermute(g, 'il', up)  3.2 us
    unnamed x12, local copies, waits for them, and re-layouts  3.11 us
    ppermute x1, starting transfers between devices, step(): odd = lax.ppermute(odd_sent, axes, odd_swap)  2.56 us
    ppermute x1, starting transfers between devices, step(): xl_got.append(lax.ppermute(buf, axes, xl_swaps[p][0]))  1.49 us
    pallas_call x1, Pallas kernels, step(): return make_update(rows, cols, steps)(rows_all, x, r, u, image)  1.36 us
    pallas_call x1, Pallas kernels, step(): part, sums = make_inner(rows, cols, steps)(u, r, s_il, s_xl, w)  1.04 us
    ppermute x1, waiting for transfers between devices, step(): xl_got.append(lax.ppermute(buf, axes, xl_swaps[p][0]))  0.98 us
  transfers between devices with their start and end apart: 4, of which 2 were waited for; matrix products, arithmetic and copies ran while one was open for 0% of the time, Pallas kernels for 5%

profile of v2, /device:TPU:0, one launch (start us, length us, event | category | flops | bytes accessed | tf_op | source)
XLA Modules:
  0.0 26.5 jit_solution(5666108425852183734)
XLA Ops:
  0.6 0.0 copy-start
  0.6 0.0 copy-start.1
  0.7 1.0 %copy-done = f32[4,64,512]{2,1,0:T(8,128)S(1)} copy-done((f32[4,64,512]{2,1,0:T(8,128)S(1)}, f32[4,64,512]{2,1,0:T(8,128)}, u32[]{:S(2)}) %copy-start) | copy-done | bytes 524312
  1.7 0.2 copy-done.1
  1.8 0.0 copy-start.4
  1.9 1.0 %copy-done.4 = f32[4,64,512]{2,1,0:T(8,128)S(1)} copy-done((f32[4,64,512]{2,1,0:T(8,128)S(1)}, f32[4,64,512]{2,1,0:T(8,128)}, u32[]{:S(2)}) %copy-start.4) | copy-done | bytes 524312
  2.9 0.1 pack.1._.rest_0_
  3.0 0.9 %copy-done.2 = f32[4,64,512]{2,1,0:T(8,128)S(1)} copy-done((f32[4,64,512]{2,1,0:T(8,128)S(1)}, f32[4,64,512]{2,1,0:T(8,128)}, u32[]{:S(2)}) %copy-start.2) | copy-done | bytes 524312
  3.9 0.1 pair.1.mine_ref._
  4.1 0.5 %collective-permute-start = (f32[2,64,512]{2,1,0:T(8,128)S(1)}, f32[2,64,512]{2,1,0:T(8,128)S(1)}, u32[]{:S(2)}, u32[]{:S(2)}) collective-permute-start(f32[2,64,512]{2,1,0:T(8,128)S(1)} %pair.1.mine_ref._), channel_id=1, source_target_pairs={{0,2},{1,3},{2,0},{3,1},{4,6},{5,7},{6,4},{7,5},{8,10},{9,11},{10,... | collective-permute-start | bytes 786440 | tf_op jit(solution)/shard_map/ppermute | solution.py:374
  4.6 2.6 %collective-permute-start.1 = (f32[64,512]{1,0:T(8,128)S(1)}, f32[64,512]{1,0:T(8,128)S(1)}, u32[]{:S(2)}, u32[]{:S(2)}) collective-permute-start(f32[64,512]{1,0:T(8,128)S(1)} %pick.1._), channel_id=1, source_target_pairs={{0,1},{1,0},{2,4},{3,5},{4,2},{5,3},{6,8},{7,9},{8,6},{9,7},{10,12... | collective-permute-start | bytes 393224 | tf_op jit(solution)/shard_map/ppermute | solution.py:368
  7.2 0.1 collective-permute-start.2
  7.3 1.5 %collective-permute-start.3 = (f32[8,512]{1,0:T(8,128)S(1)}, f32[8,512]{1,0:T(8,128)S(1)}, u32[]{:S(2)}, u32[]{:S(2)}) collective-permute-start(f32[8,512]{1,0:T(8,128)S(1)} %pack.1._.rest_0_), channel_id=1, source_target_pairs={{0,1},{2,3},{4,5},{6,7},{8,9},{10,11},{12,13},{14,15},{16,17},{18,... | collective-permute-start | bytes 49160 | tf_op jit(solution)/shard_map/ppermute | solution.py:372
  8.8 0.0 copy-done.3
  8.8 1.0 %inner.1 = (f32[4,64,512]{2,1,0:T(8,128)S(1)}, f32[4,8,512]{2,1,0:T(8,128)S(1)}) custom-call(f32[4,64,512]{2,1,0:T(8,128)S(1)} %copy-done, f32[4,64,512]{2,1,0:T(8,128)S(1)} %copy-done.3, f32[4,64,512]{2,1,0:T(8,128)S(1)} %copy-done.2, f32[4,64,512]{2,1,0:T(8,128)S(1)} %copy-done.4, f32[4,64,512]{2,1,0:T(8,128)S(1)} %copy-done.1), custom_call_target="tpu_custom_call" | custom-call | tf_op jit(solution)/shard_map/inner/pallas_call | solution.py:375
  9.9 0.0 collective-permute-done.got_ref
  9.9 0.2 even_edge.1
  10.1 1.0 %collective-permute-done.3.rest_1_ = f32[8,512]{1,0:T(8,128)S(1)} collective-permute-done((f32[8,512]{1,0:T(8,128)S(1)}, f32[8,512]{1,0:T(8,128)S(1)}, u32[]{:S(2)}, u32[]{:S(2)}) %collective-permute-start.3) | collective-permute-done | bytes 16416 | tf_op jit(solution)/shard_map/ppermute | solution.py:372
  11.1 0.0 collective-permute-done.1.odd_ref
  11.1 3.2 %collective-permute-done.2.g_ref = f32[64,512]{1,0:T(8,128)S(1)} collective-permute-done((f32[64,512]{1,0:T(8,128)S(1)}, f32[64,512]{1,0:T(8,128)S(1)}, u32[]{:S(2)}, u32[]{:S(2)}) %collective-permute-start.2) | collective-permute-done | bytes 131104 | tf_op jit(solution)/shard_map/ppermute | solution.py:366
  14.3 0.3 edges.1
  14.5 10.7 %all_to_all.11 = f32[32,1,128]{2,1,0:T(1,128)S(1)} all-to-all(f32[32,1,128]{2,1,0:T(1,128)S(1)} %bitcast.5), channel_id=1, replica_groups=mesh['il'=16,'xl'=2] {'il','xl'}, dimensions={0} | all-to-all | bytes 32768 | tf_op jit(solution)/shard_map/all_to_all | solution.py:380
  25.2 0.0 copy-done.5
  25.2 1.4 %update.1 = (f32[4,64,512]{2,1,0:T(8,128)}, f32[4,64,512]{2,1,0:T(8,128)}, f32[4,64,512]{2,1,0:T(8,128)}) custom-call(f32[32,128]{1,0:T(8,128)S(1)} %bitcast.4, f32[4,64,512]{2,1,0:T(8,128)S(1)} %copy-done.5, f32[4,64,512]{2,1,0:T(8,128)S(1)} %copy-done.3, f32[4,64,512]{2,1,0:T(8,128)S(1)} %copy-done, f32[4,64,512]{2,1,0:T(8,128)S(1)} %get-tuple-element.14.img_ref), custom_call_target="tpu_custom_call" | custom-call | tf_op jit(solution)/shard_map/update/pallas_call | solution.py:381
  (5 shorter events, 0.1 us)
Async XLA Ops:
  0.6 1.0 %copy-start = (f32[4,64,512]{2,1,0:T(8,128)S(1)}, f32[4,64,512]{2,1,0:T(8,128)}, u32[]{:S(2)}) copy-start(f32[4,64,512]{2,1,0:T(8,128)} %u_ref.13) | copy-start | bytes 1572868
  0.6 1.2 %copy-start.1 = (f32[4,64,512]{2,1,0:T(8,128)S(1)}, f32[4,64,512]{2,1,0:T(8,128)}, u32[]{:S(2)}) copy-start(f32[4,64,512]{2,1,0:T(8,128)} %w_ref.11) | copy-start | bytes 1572868
  1.8 1.0 %copy-start.4 = (f32[4,64,512]{2,1,0:T(8,128)S(1)}, f32[4,64,512]{2,1,0:T(8,128)}, u32[]{:S(2)}) copy-start(f32[4,64,512]{2,1,0:T(8,128)} %sxl_ref.5) | copy-start | bytes 1572868
  2.9 1.0 %copy-start.2 = (f32[4,64,512]{2,1,0:T(8,128)S(1)}, f32[4,64,512]{2,1,0:T(8,128)}, u32[]{:S(2)}) copy-start(f32[4,64,512]{2,1,0:T(8,128)} %sil_ref.7) | copy-start | bytes 1572868
  3.9 4.9 %copy-start.3 = (f32[4,64,512]{2,1,0:T(8,128)S(1)}, f32[4,64,512]{2,1,0:T(8,128)}, u32[]{:S(2)}) copy-start(f32[4,64,512]{2,1,0:T(8,128)} %r_ref.7) | copy-start | bytes 1572868
  4.1 5.8 %collective-permute-start = (f32[2,64,512]{2,1,0:T(8,128)S(1)}, f32[2,64,512]{2,1,0:T(8,128)S(1)}, u32[]{:S(2)}, u32[]{:S(2)}) collective-permute-start(f32[2,64,512]{2,1,0:T(8,128)S(1)} %pair.1.mine_ref._), channel_id=1, source_target_pairs={{0,2},{1,3},{2,0},{3,1},{4,6},{5,7},{6,4},{7,5},{8,10},{9,11},{10,... | collective-permute-start | bytes 786440 | tf_op jit(solution)/shard_map/ppermute | solution.py:374
  4.6 6.5 %collective-permute-start.1 = (f32[64,512]{1,0:T(8,128)S(1)}, f32[64,512]{1,0:T(8,128)S(1)}, u32[]{:S(2)}, u32[]{:S(2)}) collective-permute-start(f32[64,512]{1,0:T(8,128)S(1)} %pick.1._), channel_id=1, source_target_pairs={{0,1},{1,0},{2,4},{3,5},{4,2},{5,3},{6,8},{7,9},{8,6},{9,7},{10,12... | collective-permute-start | bytes 393224 | tf_op jit(solution)/shard_map/ppermute | solution.py:368
  7.2 7.1 %collective-permute-start.2 = (f32[64,512]{1,0:T(8,128)S(1)}, f32[64,512]{1,0:T(8,128)S(1)}, u32[]{:S(2)}, u32[]{:S(2)}) collective-permute-start(f32[64,512]{1,0:T(8,128)S(1)} %slope_row.1._.own_ref), channel_id=1, source_target_pairs={{0,2},{2,4},{4,6},{6,8},{8,10},{10,12},{12,14},{14,16},{16,18},{18... | collective-permute-start | bytes 393224 | tf_op jit(solution)/shard_map/ppermute | solution.py:366
  7.3 3.7 %collective-permute-start.3 = (f32[8,512]{1,0:T(8,128)S(1)}, f32[8,512]{1,0:T(8,128)S(1)}, u32[]{:S(2)}, u32[]{:S(2)}) collective-permute-start(f32[8,512]{1,0:T(8,128)S(1)} %pack.1._.rest_0_), channel_id=1, source_target_pairs={{0,1},{2,3},{4,5},{6,7},{8,9},{10,11},{12,13},{14,15},{16,17},{18,... | collective-permute-start | bytes 49160 | tf_op jit(solution)/shard_map/ppermute | solution.py:372
  14.3 10.9 %copy-start.5 = (f32[4,64,512]{2,1,0:T(8,128)S(1)}, f32[4,64,512]{2,1,0:T(8,128)}, u32[]{:S(2)}) copy-start(f32[4,64,512]{2,1,0:T(8,128)} %x_ref.1) | copy-start | bytes 1572868

commit v3 on v2

--- a/solution.py
+++ b/solution.py
@@ -48,32 +48,30 @@
     return jax.ShapeDtypeStruct(shape, jnp.float32)
 
 
-def make_slope_row(rows, cols, steps):
-    def kernel(u_hbm, sil_hbm, g_ref, u_ref, s_ref, sems):
+def make_rows(rows, cols, steps):
+    def kernel(w_hbm, sil_hbm, w_row, s_row, sems):
         @pl.when(lax.axis_index("il") % 2 == 1)
         def _():
-            pairs = ((u_hbm.at[rows - 1], u_ref), (sil_hbm.at[rows - 1], s_ref))
-            copies = [pltpu.make_async_copy(src, dst, sems.at[k]) for k, (src, dst) in enumerate(pairs)]
+            pairs = ((w_hbm, w_row), (sil_hbm, s_row))
+            copies = [pltpu.make_async_copy(src.at[rows - 1], dst, sems.at[k]) for k, (src, dst) in enumerate(pairs)]
             for copy in copies:
                 copy.start()
             for copy in copies:
                 copy.wait()
-            u = u_ref[...]
-            g_ref[...] = u + s_ref[...] * time_diff(u)
 
     return pl.pallas_call(
         kernel,
         in_specs=[HBM] * 2,
-        out_specs=VMEM,
-        out_shape=f32(cols, steps),
-        scratch_shapes=[pltpu.VMEM((cols, steps), jnp.float32)] * 2 + [pltpu.SemaphoreType.DMA((2,))],
-        compiler_params=params(),
-        name="slope_row",
+        out_specs=[VMEM] * 2,
+        out_shape=[f32(cols, steps)] * 2,
+        scratch_shapes=[pltpu.SemaphoreType.DMA((2,))],
+        compiler_params=params(),
+        name="rows",
     )
 
 
 def make_pick(rows, cols, steps):
-    def kernel(_, u_ref, w_ref, odd_ref):
+    def kernel(u_ref, s_row, odd_ref):
         il_odd = lax.axis_index("il") % 2
 
         @pl.when(il_odd == 0)
@@ -82,11 +80,12 @@
 
         @pl.when(il_odd == 1)
         def _():
-            odd_ref[...] = w_ref[rows - 1]
-
-    return pl.pallas_call(
-        kernel,
-        in_specs=[pl.BlockSpec(memory_space=pl.ANY), VMEM, VMEM],
+            u = u_ref[rows - 1]
+            odd_ref[...] = u + s_row[...] * time_diff(u)
+
+    return pl.pallas_call(
+        kernel,
+        in_specs=[VMEM, VMEM],
         out_specs=VMEM,
         out_shape=f32(cols, steps),
         compiler_params=params(),
@@ -208,49 +207,14 @@
     )
 
 
-def make_even_edge(rows, cols, steps, n_il):
-    def kernel(u_ref, r_ref, sil_ref, w_ref, mine_ref, got_ref, _, img_in, sums_in, img_ref, sums_ref):
-        il = lax.axis_index("il")
-
-        def add(row):
-            if rows > 1:
-                sums = add_products(
-                    [sums_ref[k] for k in range(1, 4)], [(row, j) for j in inner_tiles(cols)], u_ref, r_ref, img_ref
-                )
-                for k, value in enumerate(sums):
-                    sums_ref[k + 1] = value
-
-        @pl.when(il % 2 == 0)
-        def _():
-            @pl.when(il < n_il - 1)
-            def _():
-                img_ref[rows - 1] += lower_flux(w_ref[rows - 1], got_ref[0], mine_ref[1], sil_ref[rows - 1])
-
-            add(rows - 1)
-
-        @pl.when(il % 2 == 1)
-        def _():
-            img_ref[0] += got_ref[0] * got_ref[0] * (u_ref[0] - got_ref[1])
-            add(0)
-
-    return pl.pallas_call(
-        kernel,
-        in_specs=[VMEM] * 6 + [pl.BlockSpec(memory_space=pl.ANY)] + [VMEM] * 2,
-        out_specs=[VMEM] * 2,
-        out_shape=[f32(rows, cols, steps), f32(4, 8, steps)],
-        input_output_aliases={7: 0, 8: 1},
-        compiler_params=params(),
-        name="even_edge",
-    )
-
-
-def make_edges(rows, cols, steps, n_il, n_xl, xl_parities, n_dev):
-    def kernel(u_ref, r_ref, sil_ref, sxl_ref, w_ref, part_ref, sums_in, own_ref, odd_ref, g_ref, *rest):
-        bufs = rest[:-3]
-        img_ref, out_ref, sums_ref = rest[-3:]
+def make_near_edges(rows, cols, steps, n_il, n_xl, xl_parities):
+    half = len(xl_parities)
+
+    def kernel(u_ref, r_ref, sil_ref, sxl_ref, w_ref, img_in, sums_in, mine_ref, got_ref, *rest):
+        bufs = rest[:-2]
+        img_ref, sums_ref = rest[-2:]
         il, xl = lax.axis_index("il"), lax.axis_index("xl")
 
-        half = len(xl_parities)
         for parity, mine, got in zip(xl_parities, bufs[:half], bufs[half:]):
 
             @pl.when((xl % 2 == parity) & (xl < n_xl - 1))
@@ -267,21 +231,56 @@
                 for i in range(rows):
                     img_ref[i, pl.ds(0, 1), :] += add[i : i + 1]
 
-        def add(row):
-            tiles = [(row, j) for j in inner_tiles(cols)]
-            tiles += [(i, j) for i in range(rows) for j in edge_tiles(cols)]
+        def add_row(row):
+            tiles = [(row, j) for j in range(0, cols, 8)] if rows > 1 else []
+            tiles += [(i, j) for i in range(1, rows - 1) for j in edge_tiles(cols)]
+            sums = add_products([sums_ref[k] for k in range(1, 4)], tiles, u_ref, r_ref, img_ref)
+            for k, value in enumerate(sums):
+                sums_ref[k + 1] = value
+
+        @pl.when(il % 2 == 0)
+        def _():
+            @pl.when(il < n_il - 1)
+            def _():
+                img_ref[rows - 1] += lower_flux(w_ref[rows - 1], got_ref[0], mine_ref[1], sil_ref[rows - 1])
+
+            add_row(rows - 1)
+
+        @pl.when(il % 2 == 1)
+        def _():
+            img_ref[0] += got_ref[0] * got_ref[0] * (u_ref[0] - got_ref[1])
+            add_row(0)
+
+    return pl.pallas_call(
+        kernel,
+        in_specs=[VMEM] * (9 + 2 * half),
+        out_specs=[VMEM] * 2,
+        out_shape=[f32(rows, cols, steps), f32(4, 8, steps)],
+        input_output_aliases={5: 0, 6: 1},
+        compiler_params=params(),
+        name="near_edges",
+    )
+
+
+def make_edges(rows, cols, steps, n_il, n_dev):
+    def kernel(u_ref, r_ref, sil_ref, w_ref, img_in, sums_in, own_ref, odd_ref, w_got_ref, img_ref, out_ref, sums_ref):
+        il = lax.axis_index("il")
+
+        def add_row(row):
+            tiles = [(row, j) for j in range(0, cols, 8)]
             sums = add_products([sums_in[k] for k in range(1, 4)], tiles, u_ref, r_ref, img_ref)
-            for k, value in enumerate(sums):
-                sums_ref[k] = value
+            for k, value in enumerate([sums_in[0]] + sums):
+                value = sum(value[:, j : j + 128] for j in range(128, steps, 128)) + value[:, :128]
+                sums_ref[pl.ds(k, 1)] = jnp.sum(value, axis=0, keepdims=True)
 
         @pl.when(il % 2 == 0)
         def _():
             @pl.when(il > 0)
             def _():
-                w = odd_ref[...]
-                img_ref[0] += w * w * (u_ref[0] - g_ref[...])
-
-            add(0)
+                w = w_got_ref[...]
+                img_ref[0] += w * w * (u_ref[0] - odd_ref[...])
+
+            add_row(0)
 
         @pl.when(il % 2 == 1)
         def _():
@@ -289,23 +288,21 @@
             def _():
                 img_ref[rows - 1] += lower_flux(w_ref[rows - 1], odd_ref[...], own_ref[...], sil_ref[rows - 1])
 
-            add(rows - 1)
+            add_row(rows - 1)
 
         lane = lax.broadcasted_iota(jnp.int32, (1, 128), 1)
         row = jnp.zeros((1, 128), jnp.float32)
-        for k, value in enumerate([sums_in[0]] + [sums_ref[k] for k in range(3)]):
-            value = sum(value[:, j : j + 128] for j in range(128, steps, 128)) + value[:, :128]
-            value = jnp.sum(jnp.sum(value, axis=0, keepdims=True), axis=1, keepdims=True)
-            row = jnp.where(lane == k, value, row)
+        for k in range(4):
+            row = jnp.where(lane == k, jnp.sum(sums_ref[pl.ds(k, 1)], axis=1, keepdims=True), row)
         out_ref[...] = jnp.broadcast_to(row, (n_dev, 128))
 
     return pl.pallas_call(
         kernel,
-        in_specs=[VMEM] * (10 + 2 * len(xl_parities)),
+        in_specs=[VMEM] * 9,
         out_specs=[VMEM, VMEM],
         out_shape=[f32(rows, cols, steps), f32(n_dev, 128)],
-        input_output_aliases={5: 0},
-        scratch_shapes=[pltpu.VMEM((3, 8, steps), jnp.float32)],
+        input_output_aliases={4: 0},
+        scratch_shapes=[pltpu.VMEM((4, 128), jnp.float32)],
         compiler_params=params(),
         name="edges",
     )
@@ -361,10 +358,10 @@
 
     def step(x, r, u, s_il, s_xl, w):
         rows, cols, steps = u.shape
-        stay = [pltpu.with_memory_space_constraint(a, pltpu.HBM) for a in (u, s_il)]
-        g = make_slope_row(rows, cols, steps)(stay[0], stay[1])
-        g_got = lax.ppermute(g, "il", up)
-        odd_sent = make_pick(rows, cols, steps)(g, u, w)
+        stay = [pltpu.with_memory_space_constraint(a, pltpu.HBM) for a in (w, s_il)]
+        w_sent, s_row = make_rows(rows, cols, steps)(*stay)
+        w_got = lax.ppermute(w_sent, "il", up)
+        odd_sent = make_pick(rows, cols, steps)(u, s_row)
         odd = lax.ppermute(odd_sent, axes, odd_swap)
         xl_sent = make_pack(rows, cols, steps, xl_parities)(odd_sent, u, s_xl, w)
         xl_got = []
@@ -373,10 +370,10 @@
         even_sent = make_pair(rows, cols, steps)(xl_sent[0] if xl_sent else odd_sent, u, s_il, w)
         even = lax.ppermute(even_sent, axes, even_swap)
         part, sums = make_inner(rows, cols, steps)(u, r, s_il, s_xl, w)
-        part, sums = make_even_edge(rows, cols, steps, n_il)(u, r, s_il, w, even_sent, even, even_sent, part, sums)
-        image, row = make_edges(rows, cols, steps, n_il, n_xl, xl_parities, n_dev)(
-            u, r, s_il, s_xl, w, part, sums, g, odd, g_got, *xl_sent, *xl_got
+        part, sums = make_near_edges(rows, cols, steps, n_il, n_xl, xl_parities)(
+            u, r, s_il, s_xl, w, part, sums, even_sent, even, *xl_sent, *xl_got
         )
+        image, row = make_edges(rows, cols, steps, n_il, n_dev)(u, r, s_il, w, part, sums, odd_sent, odd, w_got)
         rows_all = lax.all_to_all(row, axes, 0, 0, tiled=True)
         return make_update(rows, cols, steps)(rows_all, x, r, u, image)
 

time: 26.8 us -> 26.1 us (0.974)
  local copies, waits for them, and re-layouts: 3.11 us -> 2.24 us
  starting transfers between devices: 4.74 us -> 5.2 us
    unnamed x12, local copies, waits for them, and re-layouts: 3.11 us -> 2.24 us
    ppermute x1, starting transfers between devices: 0.55 us -> 1.25 us  [step(): even = lax.ppermute(even_sent, axes, even_swap)]
    ppermute x1, waiting for transfers between devices: 3.2 us -> 2.88 us  [step(): w_got = lax.ppermute(w_sent, 'il', up)]
where the time goes in v3:
time: 26.1 us; the launch traced here: 25.9 us
  blocking collectives  10.5 us (40%)
  starting transfers between devices  5.2 us (20%)
  waiting for transfers between devices  4.08 us (16%)
  Pallas kernels  3.11 us (12%)
  local copies, waits for them, and re-layouts  2.24 us (9%)
  between operations  0.72 us (3%)
    all_to_all x1, blocking collectives, step(): rows_all = lax.all_to_all(row, axes, 0, 0, tiled=True)  10.5 us
    ppermute x1, waiting for transfers between devices, step(): w_got = lax.ppermute(w_sent, 'il', up)  2.88 us
    ppermute x1, starting transfers between devices, step(): odd = lax.ppermute(odd_sent, axes, odd_swap)  2.31 us
    unnamed x12, local copies, waits for them, and re-layouts  2.24 us
    ppermute x1, starting transfers between devices, step(): xl_got.append(lax.ppermute(buf, axes, xl_swaps[p][0]))  1.49 us
    pallas_call x1, Pallas kernels, step(): return make_update(rows, cols, steps)(rows_all, x, r, u, image)  1.36 us
    ppermute x1, starting transfers between devices, step(): even = lax.ppermute(even_sent, axes, even_swap)  1.25 us
    ppermute x1, waiting for transfers between devices, step(): xl_got.append(lax.ppermute(buf, axes, xl_swaps[p][0]))  1.19 us
  transfers between devices with their start and end apart: 4, of which 2 were waited for; matrix products, arithmetic and copies ran while one was open for 0% of the time, Pallas kernels for 5%

profile of v3, /device:TPU:0, one launch (start us, length us, event | category | flops | bytes accessed | tf_op | source)
XLA Modules:
  0.0 25.9 jit_solution(10541853611273207206)
XLA Ops:
  0.6 0.0 copy-start
  0.6 0.0 copy-start.4
  0.7 0.0 copy-start.1
  0.7 1.0 %copy-done = f32[4,64,512]{2,1,0:T(8,128)S(1)} copy-done((f32[4,64,512]{2,1,0:T(8,128)S(1)}, f32[4,64,512]{2,1,0:T(8,128)}, u32[]{:S(2)}) %copy-start) | copy-done | bytes 524312
  1.7 0.1 copy-done.4
  1.8 0.2 copy-done.1
  2.0 0.1 pack.1._.rest_0_
  2.1 0.9 %copy-done.2 = f32[4,64,512]{2,1,0:T(8,128)S(1)} copy-done((f32[4,64,512]{2,1,0:T(8,128)S(1)}, f32[4,64,512]{2,1,0:T(8,128)}, u32[]{:S(2)}) %copy-start.2) | copy-done | bytes 524312
  3.0 0.1 pair.1.mine_ref
  3.2 1.3 %collective-permute-start = (f32[2,64,512]{2,1,0:T(8,128)S(1)}, f32[2,64,512]{2,1,0:T(8,128)S(1)}, u32[]{:S(2)}, u32[]{:S(2)}) collective-permute-start(f32[2,64,512]{2,1,0:T(8,128)S(1)} %pair.1.mine_ref), channel_id=1, source_target_pairs={{0,2},{1,3},{2,0},{3,1},{4,6},{5,7},{6,4},{7,5},{8,10},{9,11},{10,... | collective-permute-start | bytes 786440 | tf_op jit(solution)/shard_map/ppermute | solution.py:371
  4.5 2.3 %collective-permute-start.2 = (f32[64,512]{1,0:T(8,128)S(1)}, f32[64,512]{1,0:T(8,128)S(1)}, u32[]{:S(2)}, u32[]{:S(2)}) collective-permute-start(f32[64,512]{1,0:T(8,128)S(1)} %pick.1._.own_ref), channel_id=1, source_target_pairs={{0,1},{1,0},{2,4},{3,5},{4,2},{5,3},{6,8},{7,9},{8,6},{9,7},{10,12... | collective-permute-start | bytes 393224 | tf_op jit(solution)/shard_map/ppermute | solution.py:365
  6.8 0.1 collective-permute-start.3
  6.9 1.5 %collective-permute-start.1 = (f32[8,512]{1,0:T(8,128)S(1)}, f32[8,512]{1,0:T(8,128)S(1)}, u32[]{:S(2)}, u32[]{:S(2)}) collective-permute-start(f32[8,512]{1,0:T(8,128)S(1)} %pack.1._.rest_0_), channel_id=1, source_target_pairs={{0,1},{2,3},{4,5},{6,7},{8,9},{10,11},{12,13},{14,15},{16,17},{18,... | collective-permute-start | bytes 49160 | tf_op jit(solution)/shard_map/ppermute | solution.py:369
  8.4 0.0 copy-done.3
  8.4 1.0 %inner.1 = (f32[4,64,512]{2,1,0:T(8,128)S(1)}, f32[4,8,512]{2,1,0:T(8,128)S(1)}) custom-call(f32[4,64,512]{2,1,0:T(8,128)S(1)} %copy-done, f32[4,64,512]{2,1,0:T(8,128)S(1)} %copy-done.3, f32[4,64,512]{2,1,0:T(8,128)S(1)} %copy-done.2, f32[4,64,512]{2,1,0:T(8,128)S(1)} %copy-done.4, f32[4,64,512]{2,1,0:T(8,128)S(1)} %copy-done.1), custom_call_target="tpu_custom_call" | custom-call | tf_op jit(solution)/shard_map/inner/pallas_call | solution.py:372
  9.5 1.2 %collective-permute-done.1.rest_1_ = f32[8,512]{1,0:T(8,128)S(1)} collective-permute-done((f32[8,512]{1,0:T(8,128)S(1)}, f32[8,512]{1,0:T(8,128)S(1)}, u32[]{:S(2)}, u32[]{:S(2)}) %collective-permute-start.1) | collective-permute-done | bytes 16416 | tf_op jit(solution)/shard_map/ppermute | solution.py:369
  10.6 0.0 collective-permute-done.got_ref
  10.7 0.3 %near_edges.1 = (f32[4,64,512]{2,1,0:T(8,128)S(1)}, f32[4,8,512]{2,1,0:T(8,128)S(1)}) custom-call(f32[4,64,512]{2,1,0:T(8,128)S(1)} %copy-done, f32[4,64,512]{2,1,0:T(8,128)S(1)} %copy-done.3, f32[4,64,512]{2,1,0:T(8,128)S(1)} %copy-done.2, f32[4,64,512]{2,1,0:T(8,128)S(1)} %copy-done.4, ...), custom_call_target="tpu_custom_call", output_to_operand_aliasing={{0}: (5, {}), {1}: (6, {})} | custom-call | tf_op jit(solution)/shard_map/near_edges/pallas_call | solution.py:373
  11.0 0.0 collective-permute-done.2.odd_ref
  11.0 2.9 %collective-permute-done.3.w_got_ref = f32[64,512]{1,0:T(8,128)S(1)} collective-permute-done((f32[64,512]{1,0:T(8,128)S(1)}, f32[64,512]{1,0:T(8,128)S(1)}, u32[]{:S(2)}, u32[]{:S(2)}) %collective-permute-start.3) | collective-permute-done | bytes 131104 | tf_op jit(solution)/shard_map/ppermute | solution.py:363
  13.9 0.1 edges.1
  14.0 10.5 %all_to_all.11 = f32[32,1,128]{2,1,0:T(1,128)S(1)} all-to-all(f32[32,1,128]{2,1,0:T(1,128)S(1)} %bitcast.5), channel_id=1, replica_groups=mesh['il'=16,'xl'=2] {'il','xl'}, dimensions={0} | all-to-all | bytes 32768 | tf_op jit(solution)/shard_map/all_to_all | solution.py:377
  24.5 0.0 copy-done.5
  24.5 1.4 %update.1 = (f32[4,64,512]{2,1,0:T(8,128)}, f32[4,64,512]{2,1,0:T(8,128)}, f32[4,64,512]{2,1,0:T(8,128)}) custom-call(f32[32,128]{1,0:T(8,128)S(1)} %bitcast.4, f32[4,64,512]{2,1,0:T(8,128)S(1)} %copy-done.5, f32[4,64,512]{2,1,0:T(8,128)S(1)} %copy-done.3, f32[4,64,512]{2,1,0:T(8,128)S(1)} %copy-done, f32[4,64,512]{2,1,0:T(8,128)S(1)} %get-tuple-element.18.img_ref), custom_call_target="tpu_custom_call" | custom-call | tf_op jit(solution)/shard_map/update/pallas_call | solution.py:378
  (5 shorter events, 0.1 us)
Async XLA Ops:
  0.6 1.0 %copy-start = (f32[4,64,512]{2,1,0:T(8,128)S(1)}, f32[4,64,512]{2,1,0:T(8,128)}, u32[]{:S(2)}) copy-start(f32[4,64,512]{2,1,0:T(8,128)} %u_ref.13) | copy-start | bytes 1572868
  0.6 1.2 %copy-start.4 = (f32[4,64,512]{2,1,0:T(8,128)S(1)}, f32[4,64,512]{2,1,0:T(8,128)}, u32[]{:S(2)}) copy-start(f32[4,64,512]{2,1,0:T(8,128)} %sxl_ref.5) | copy-start | bytes 1572868
  0.7 1.3 %copy-start.1 = (f32[4,64,512]{2,1,0:T(8,128)S(1)}, f32[4,64,512]{2,1,0:T(8,128)}, u32[]{:S(2)}) copy-start(f32[4,64,512]{2,1,0:T(8,128)} %w_ref.9) | copy-start | bytes 1572868
  2.0 1.0 %copy-start.2 = (f32[4,64,512]{2,1,0:T(8,128)S(1)}, f32[4,64,512]{2,1,0:T(8,128)}, u32[]{:S(2)}) copy-start(f32[4,64,512]{2,1,0:T(8,128)} %sil_ref.7) | copy-start | bytes 1572868
  3.0 5.4 %copy-start.3 = (f32[4,64,512]{2,1,0:T(8,128)S(1)}, f32[4,64,512]{2,1,0:T(8,128)}, u32[]{:S(2)}) copy-start(f32[4,64,512]{2,1,0:T(8,128)} %r_ref.7) | copy-start | bytes 1572868
  3.2 7.5 %collective-permute-start = (f32[2,64,512]{2,1,0:T(8,128)S(1)}, f32[2,64,512]{2,1,0:T(8,128)S(1)}, u32[]{:S(2)}, u32[]{:S(2)}) collective-permute-start(f32[2,64,512]{2,1,0:T(8,128)S(1)} %pair.1.mine_ref), channel_id=1, source_target_pairs={{0,2},{1,3},{2,0},{3,1},{4,6},{5,7},{6,4},{7,5},{8,10},{9,11},{10,... | collective-permute-start | bytes 786440 | tf_op jit(solution)/shard_map/ppermute | solution.py:371
  4.5 6.5 %collective-permute-start.2 = (f32[64,512]{1,0:T(8,128)S(1)}, f32[64,512]{1,0:T(8,128)S(1)}, u32[]{:S(2)}, u32[]{:S(2)}) collective-permute-start(f32[64,512]{1,0:T(8,128)S(1)} %pick.1._.own_ref), channel_id=1, source_target_pairs={{0,1},{1,0},{2,4},{3,5},{4,2},{5,3},{6,8},{7,9},{8,6},{9,7},{10,12... | collective-permute-start | bytes 393224 | tf_op jit(solution)/shard_map/ppermute | solution.py:365
  6.8 7.1 %collective-permute-start.3 = (f32[64,512]{1,0:T(8,128)S(1)}, f32[64,512]{1,0:T(8,128)S(1)}, u32[]{:S(2)}, u32[]{:S(2)}) collective-permute-start(f32[64,512]{1,0:T(8,128)S(1)} %get-tuple-element.16), channel_id=1, source_target_pairs={{0,2},{2,4},{4,6},{6,8},{8,10},{10,12},{12,14},{14,16},{16,18},{18... | collective-permute-start | bytes 393224 | tf_op jit(solution)/shard_map/ppermute | solution.py:363
  6.9 3.7 %collective-permute-start.1 = (f32[8,512]{1,0:T(8,128)S(1)}, f32[8,512]{1,0:T(8,128)S(1)}, u32[]{:S(2)}, u32[]{:S(2)}) collective-permute-start(f32[8,512]{1,0:T(8,128)S(1)} %pack.1._.rest_0_), channel_id=1, source_target_pairs={{0,1},{2,3},{4,5},{6,7},{8,9},{10,11},{12,13},{14,15},{16,17},{18,... | collective-permute-start | bytes 49160 | tf_op jit(solution)/shard_map/ppermute | solution.py:369
  13.9 10.6 %copy-start.5 = (f32[4,64,512]{2,1,0:T(8,128)S(1)}, f32[4,64,512]{2,1,0:T(8,128)}, u32[]{:S(2)}) copy-start(f32[4,64,512]{2,1,0:T(8,128)} %x_ref.1) | copy-start | bytes 1572868

commit v4 on v2

--- a/solution.py
+++ b/solution.py
@@ -295,8 +295,9 @@
         row = jnp.zeros((1, 128), jnp.float32)
         for k, value in enumerate([sums_in[0]] + [sums_ref[k] for k in range(3)]):
             value = sum(value[:, j : j + 128] for j in range(128, steps, 128)) + value[:, :128]
-            value = jnp.sum(jnp.sum(value, axis=0, keepdims=True), axis=1, keepdims=True)
-            row = jnp.where(lane == k, value, row)
+            value = jnp.sum(value, axis=0, keepdims=True)
+            value = value + pltpu.roll(value, 64, 1)
+            row = jnp.where(lane // 32 == k, value + pltpu.roll(value, 32, 1), row)
         out_ref[...] = jnp.broadcast_to(row, (n_dev, 128))
 
     return pl.pallas_call(
@@ -318,7 +319,7 @@
         total = jnp.sum(sums_ref[...], axis=0, keepdims=True)
         lane = lax.broadcasted_iota(jnp.int32, total.shape, 1)
         norm_old, along, cross, square = (
-            jnp.sum(jnp.where(lane == k, total, 0.0), axis=1, keepdims=True) for k in range(4)
+            jnp.sum(jnp.where(lane // 32 == k, total, 0.0), axis=1, keepdims=True) for k in range(4)
         )
         alpha = norm_old / along
         norm_new = norm_old - 2.0 * alpha * cross + alpha * alpha * square

time: 26.8 us -> 26.9 us (level)
  no operation moved by 1% of the time
where the time goes in v4:
time: 26.9 us; the launch traced here: 26.6 us
  blocking collectives  10.7 us (40%)
  starting transfers between devices  4.74 us (18%)
  waiting for transfers between devices  4.18 us (16%)
  Pallas kernels  3.2 us (12%)
  local copies, waits for them, and re-layouts  3.11 us (12%)
  between operations  0.71 us (3%)
    all_to_all x1, blocking collectives, step(): rows_all = lax.all_to_all(row, axes, 0, 0, tiled=True)  10.7 us
    ppermute x1, waiting for transfers between devices, step(): g_got = lax.ppermute(g, 'il', up)  3.2 us
    unnamed x12, local copies, waits for them, and re-layouts  3.11 us
    ppermute x1, starting transfers between devices, step(): odd = lax.ppermute(odd_sent, axes, odd_swap)  2.56 us
    ppermute x1, starting transfers between devices, step(): xl_got.append(lax.ppermute(buf, axes, xl_swaps[p][0]))  1.49 us
    pallas_call x1, Pallas kernels, step(): return make_update(rows, cols, steps)(rows_all, x, r, u, image)  1.36 us
    pallas_call x1, Pallas kernels, step(): part, sums = make_inner(rows, cols, steps)(u, r, s_il, s_xl, w)  1.04 us
    ppermute x1, waiting for transfers between devices, step(): xl_got.append(lax.ppermute(buf, axes, xl_swaps[p][0]))  0.98 us
  transfers between devices with their start and end apart: 4, of which 2 were waited for; matrix products, arithmetic and copies ran while one was open for 0% of the time, Pallas kernels for 5%

profile of v4, /device:TPU:0, one launch (start us, length us, event | category | flops | bytes accessed | tf_op | source)
XLA Modules:
  0.0 26.6 jit_solution(227456734557936241)
XLA Ops:
  0.6 0.0 copy-start
  0.6 0.0 copy-start.1
  0.7 1.0 %copy-done = f32[4,64,512]{2,1,0:T(8,128)S(1)} copy-done((f32[4,64,512]{2,1,0:T(8,128)S(1)}, f32[4,64,512]{2,1,0:T(8,128)}, u32[]{:S(2)}) %copy-start) | copy-done | bytes 524312
  1.7 0.2 copy-done.1
  1.8 0.0 copy-start.4
  1.9 1.0 %copy-done.4 = f32[4,64,512]{2,1,0:T(8,128)S(1)} copy-done((f32[4,64,512]{2,1,0:T(8,128)S(1)}, f32[4,64,512]{2,1,0:T(8,128)}, u32[]{:S(2)}) %copy-start.4) | copy-done | bytes 524312
  2.9 0.1 pack.1._.rest_0_
  3.0 0.9 %copy-done.2 = f32[4,64,512]{2,1,0:T(8,128)S(1)} copy-done((f32[4,64,512]{2,1,0:T(8,128)S(1)}, f32[4,64,512]{2,1,0:T(8,128)}, u32[]{:S(2)}) %copy-start.2) | copy-done | bytes 524312
  3.9 0.1 pair.1.mine_ref._
  4.1 0.5 %collective-permute-start = (f32[2,64,512]{2,1,0:T(8,128)S(1)}, f32[2,64,512]{2,1,0:T(8,128)S(1)}, u32[]{:S(2)}, u32[]{:S(2)}) collective-permute-start(f32[2,64,512]{2,1,0:T(8,128)S(1)} %pair.1.mine_ref._), channel_id=1, source_target_pairs={{0,2},{1,3},{2,0},{3,1},{4,6},{5,7},{6,4},{7,5},{8,10},{9,11},{10,... | collective-permute-start | bytes 786440 | tf_op jit(solution)/shard_map/ppermute | solution.py:375
  4.6 2.6 %collective-permute-start.1 = (f32[64,512]{1,0:T(8,128)S(1)}, f32[64,512]{1,0:T(8,128)S(1)}, u32[]{:S(2)}, u32[]{:S(2)}) collective-permute-start(f32[64,512]{1,0:T(8,128)S(1)} %pick.1._), channel_id=1, source_target_pairs={{0,1},{1,0},{2,4},{3,5},{4,2},{5,3},{6,8},{7,9},{8,6},{9,7},{10,12... | collective-permute-start | bytes 393224 | tf_op jit(solution)/shard_map/ppermute | solution.py:369
  7.2 0.1 collective-permute-start.2
  7.3 1.5 %collective-permute-start.3 = (f32[8,512]{1,0:T(8,128)S(1)}, f32[8,512]{1,0:T(8,128)S(1)}, u32[]{:S(2)}, u32[]{:S(2)}) collective-permute-start(f32[8,512]{1,0:T(8,128)S(1)} %pack.1._.rest_0_), channel_id=1, source_target_pairs={{0,1},{2,3},{4,5},{6,7},{8,9},{10,11},{12,13},{14,15},{16,17},{18,... | collective-permute-start | bytes 49160 | tf_op jit(solution)/shard_map/ppermute | solution.py:373
  8.8 0.0 copy-done.3
  8.8 1.0 %inner.1 = (f32[4,64,512]{2,1,0:T(8,128)S(1)}, f32[4,8,512]{2,1,0:T(8,128)S(1)}) custom-call(f32[4,64,512]{2,1,0:T(8,128)S(1)} %copy-done, f32[4,64,512]{2,1,0:T(8,128)S(1)} %copy-done.3, f32[4,64,512]{2,1,0:T(8,128)S(1)} %copy-done.2, f32[4,64,512]{2,1,0:T(8,128)S(1)} %copy-done.4, f32[4,64,512]{2,1,0:T(8,128)S(1)} %copy-done.1), custom_call_target="tpu_custom_call" | custom-call | tf_op jit(solution)/shard_map/inner/pallas_call | solution.py:376
  9.9 0.0 collective-permute-done.got_ref
  9.9 0.2 even_edge.1
  10.1 1.0 %collective-permute-done.3.rest_1_ = f32[8,512]{1,0:T(8,128)S(1)} collective-permute-done((f32[8,512]{1,0:T(8,128)S(1)}, f32[8,512]{1,0:T(8,128)S(1)}, u32[]{:S(2)}, u32[]{:S(2)}) %collective-permute-start.3) | collective-permute-done | bytes 16416 | tf_op jit(solution)/shard_map/ppermute | solution.py:373
  11.1 0.0 collective-permute-done.1.odd_ref
  11.1 3.2 %collective-permute-done.2.g_ref = f32[64,512]{1,0:T(8,128)S(1)} collective-permute-done((f32[64,512]{1,0:T(8,128)S(1)}, f32[64,512]{1,0:T(8,128)S(1)}, u32[]{:S(2)}, u32[]{:S(2)}) %collective-permute-start.2) | collective-permute-done | bytes 131104 | tf_op jit(solution)/shard_map/ppermute | solution.py:367
  14.3 0.3 %edges.1 = (f32[4,64,512]{2,1,0:T(8,128)S(1)}, f32[32,128]{1,0:T(8,128)S(1)}) custom-call(f32[4,64,512]{2,1,0:T(8,128)S(1)} %copy-done, f32[4,64,512]{2,1,0:T(8,128)S(1)} %copy-done.3, f32[4,64,512]{2,1,0:T(8,128)S(1)} %copy-done.2, f32[4,64,512]{2,1,0:T(8,128)S(1)} %copy-done.4, f32[4,64,512]{2,1,0:T(8,128)S(1)} %copy-done.1, ...), custom_call_target="tpu_custom_call", output_to_operand_aliasing={{0}: (5, {})} | custom-call | tf_op jit(solution)/shard_map/edges/pallas_call | solution.py:378
  14.6 10.7 %all_to_all.11 = f32[32,1,128]{2,1,0:T(1,128)S(1)} all-to-all(f32[32,1,128]{2,1,0:T(1,128)S(1)} %bitcast.5), channel_id=1, replica_groups=mesh['il'=16,'xl'=2] {'il','xl'}, dimensions={0} | all-to-all | bytes 32768 | tf_op jit(solution)/shard_map/all_to_all | solution.py:381
  25.2 0.0 copy-done.5
  25.2 1.4 %update.1 = (f32[4,64,512]{2,1,0:T(8,128)}, f32[4,64,512]{2,1,0:T(8,128)}, f32[4,64,512]{2,1,0:T(8,128)}) custom-call(f32[32,128]{1,0:T(8,128)S(1)} %bitcast.4, f32[4,64,512]{2,1,0:T(8,128)S(1)} %copy-done.5, f32[4,64,512]{2,1,0:T(8,128)S(1)} %copy-done.3, f32[4,64,512]{2,1,0:T(8,128)S(1)} %copy-done, f32[4,64,512]{2,1,0:T(8,128)S(1)} %get-tuple-element.14.img_ref), custom_call_target="tpu_custom_call" | custom-call | tf_op jit(solution)/shard_map/update/pallas_call | solution.py:382
  (5 shorter events, 0.1 us)
Async XLA Ops:
  0.6 1.0 %copy-start = (f32[4,64,512]{2,1,0:T(8,128)S(1)}, f32[4,64,512]{2,1,0:T(8,128)}, u32[]{:S(2)}) copy-start(f32[4,64,512]{2,1,0:T(8,128)} %u_ref.13) | copy-start | bytes 1572868
  0.6 1.2 %copy-start.1 = (f32[4,64,512]{2,1,0:T(8,128)S(1)}, f32[4,64,512]{2,1,0:T(8,128)}, u32[]{:S(2)}) copy-start(f32[4,64,512]{2,1,0:T(8,128)} %w_ref.11) | copy-start | bytes 1572868
  1.8 1.0 %copy-start.4 = (f32[4,64,512]{2,1,0:T(8,128)S(1)}, f32[4,64,512]{2,1,0:T(8,128)}, u32[]{:S(2)}) copy-start(f32[4,64,512]{2,1,0:T(8,128)} %sxl_ref.5) | copy-start | bytes 1572868
  2.9 1.0 %copy-start.2 = (f32[4,64,512]{2,1,0:T(8,128)S(1)}, f32[4,64,512]{2,1,0:T(8,128)}, u32[]{:S(2)}) copy-start(f32[4,64,512]{2,1,0:T(8,128)} %sil_ref.7) | copy-start | bytes 1572868
  3.9 4.9 %copy-start.3 = (f32[4,64,512]{2,1,0:T(8,128)S(1)}, f32[4,64,512]{2,1,0:T(8,128)}, u32[]{:S(2)}) copy-start(f32[4,64,512]{2,1,0:T(8,128)} %r_ref.7) | copy-start | bytes 1572868
  4.1 5.8 %collective-permute-start = (f32[2,64,512]{2,1,0:T(8,128)S(1)}, f32[2,64,512]{2,1,0:T(8,128)S(1)}, u32[]{:S(2)}, u32[]{:S(2)}) collective-permute-start(f32[2,64,512]{2,1,0:T(8,128)S(1)} %pair.1.mine_ref._), channel_id=1, source_target_pairs={{0,2},{1,3},{2,0},{3,1},{4,6},{5,7},{6,4},{7,5},{8,10},{9,11},{10,... | collective-permute-start | bytes 786440 | tf_op jit(solution)/shard_map/ppermute | solution.py:375
  4.6 6.5 %collective-permute-start.1 = (f32[64,512]{1,0:T(8,128)S(1)}, f32[64,512]{1,0:T(8,128)S(1)}, u32[]{:S(2)}, u32[]{:S(2)}) collective-permute-start(f32[64,512]{1,0:T(8,128)S(1)} %pick.1._), channel_id=1, source_target_pairs={{0,1},{1,0},{2,4},{3,5},{4,2},{5,3},{6,8},{7,9},{8,6},{9,7},{10,12... | collective-permute-start | bytes 393224 | tf_op jit(solution)/shard_map/ppermute | solution.py:369
  7.2 7.1 %collective-permute-start.2 = (f32[64,512]{1,0:T(8,128)S(1)}, f32[64,512]{1,0:T(8,128)S(1)}, u32[]{:S(2)}, u32[]{:S(2)}) collective-permute-start(f32[64,512]{1,0:T(8,128)S(1)} %slope_row.1._.own_ref), channel_id=1, source_target_pairs={{0,2},{2,4},{4,6},{6,8},{8,10},{10,12},{12,14},{14,16},{16,18},{18... | collective-permute-start | bytes 393224 | tf_op jit(solution)/shard_map/ppermute | solution.py:367
  7.3 3.7 %collective-permute-start.3 = (f32[8,512]{1,0:T(8,128)S(1)}, f32[8,512]{1,0:T(8,128)S(1)}, u32[]{:S(2)}, u32[]{:S(2)}) collective-permute-start(f32[8,512]{1,0:T(8,128)S(1)} %pack.1._.rest_0_), channel_id=1, source_target_pairs={{0,1},{2,3},{4,5},{6,7},{8,9},{10,11},{12,13},{14,15},{16,17},{18,... | collective-permute-start | bytes 49160 | tf_op jit(solution)/shard_map/ppermute | solution.py:373
  14.3 11.0 %copy-start.5 = (f32[4,64,512]{2,1,0:T(8,128)S(1)}, f32[4,64,512]{2,1,0:T(8,128)}, u32[]{:S(2)}) copy-start(f32[4,64,512]{2,1,0:T(8,128)} %x_ref.1) | copy-start | bytes 1572868

commit v5 on v3

--- a/solution.py
+++ b/solution.py
@@ -48,30 +48,32 @@
     return jax.ShapeDtypeStruct(shape, jnp.float32)
 
 
-def make_rows(rows, cols, steps):
-    def kernel(w_hbm, sil_hbm, w_row, s_row, sems):
+def make_slope_row(rows, cols, steps):
+    def kernel(u_hbm, sil_hbm, g_ref, u_ref, s_ref, sems):
         @pl.when(lax.axis_index("il") % 2 == 1)
         def _():
-            pairs = ((w_hbm, w_row), (sil_hbm, s_row))
-            copies = [pltpu.make_async_copy(src.at[rows - 1], dst, sems.at[k]) for k, (src, dst) in enumerate(pairs)]
+            pairs = ((u_hbm.at[rows - 1], u_ref), (sil_hbm.at[rows - 1], s_ref))
+            copies = [pltpu.make_async_copy(src, dst, sems.at[k]) for k, (src, dst) in enumerate(pairs)]
             for copy in copies:
                 copy.start()
             for copy in copies:
                 copy.wait()
+            u = u_ref[...]
+            g_ref[...] = u + s_ref[...] * time_diff(u)
 
     return pl.pallas_call(
         kernel,
         in_specs=[HBM] * 2,
-        out_specs=[VMEM] * 2,
-        out_shape=[f32(cols, steps)] * 2,
-        scratch_shapes=[pltpu.SemaphoreType.DMA((2,))],
-        compiler_params=params(),
-        name="rows",
+        out_specs=VMEM,
+        out_shape=f32(cols, steps),
+        scratch_shapes=[pltpu.VMEM((cols, steps), jnp.float32)] * 2 + [pltpu.SemaphoreType.DMA((2,))],
+        compiler_params=params(),
+        name="slope_row",
     )
 
 
 def make_pick(rows, cols, steps):
-    def kernel(u_ref, s_row, odd_ref):
+    def kernel(_, u_ref, w_ref, odd_ref):
         il_odd = lax.axis_index("il") % 2
 
         @pl.when(il_odd == 0)
@@ -80,12 +82,11 @@
 
         @pl.when(il_odd == 1)
         def _():
-            u = u_ref[rows - 1]
-            odd_ref[...] = u + s_row[...] * time_diff(u)
-
-    return pl.pallas_call(
-        kernel,
-        in_specs=[VMEM, VMEM],
+            odd_ref[...] = w_ref[rows - 1]
+
+    return pl.pallas_call(
+        kernel,
+        in_specs=[pl.BlockSpec(memory_space=pl.ANY), VMEM, VMEM],
         out_specs=VMEM,
         out_shape=f32(cols, steps),
         compiler_params=params(),
@@ -263,7 +264,7 @@
 
 
 def make_edges(rows, cols, steps, n_il, n_dev):
-    def kernel(u_ref, r_ref, sil_ref, w_ref, img_in, sums_in, own_ref, odd_ref, w_got_ref, img_ref, out_ref, sums_ref):
+    def kernel(u_ref, r_ref, sil_ref, w_ref, img_in, sums_in, own_ref, odd_ref, g_ref, img_ref, out_ref, sums_ref):
         il = lax.axis_index("il")
 
         def add_row(row):
@@ -277,8 +278,8 @@
         def _():
             @pl.when(il > 0)
             def _():
-                w = w_got_ref[...]
-                img_ref[0] += w * w * (u_ref[0] - odd_ref[...])
+                w = odd_ref[...]
+                img_ref[0] += w * w * (u_ref[0] - g_ref[...])
 
             add_row(0)
 
@@ -358,10 +359,10 @@
 
     def step(x, r, u, s_il, s_xl, w):
         rows, cols, steps = u.shape
-        stay = [pltpu.with_memory_space_constraint(a, pltpu.HBM) for a in (w, s_il)]
-        w_sent, s_row = make_rows(rows, cols, steps)(*stay)
-        w_got = lax.ppermute(w_sent, "il", up)
-        odd_sent = make_pick(rows, cols, steps)(u, s_row)
+        stay = [pltpu.with_memory_space_constraint(a, pltpu.HBM) for a in (u, s_il)]
+        g = make_slope_row(rows, cols, steps)(stay[0], stay[1])
+        g_got = lax.ppermute(g, "il", up)
+        odd_sent = make_pick(rows, cols, steps)(g, u, w)
         odd = lax.ppermute(odd_sent, axes, odd_swap)
         xl_sent = make_pack(rows, cols, steps, xl_parities)(odd_sent, u, s_xl, w)
         xl_got = []
@@ -373,7 +374,7 @@
         part, sums = make_near_edges(rows, cols, steps, n_il, n_xl, xl_parities)(
             u, r, s_il, s_xl, w, part, sums, even_sent, even, *xl_sent, *xl_got
         )
-        image, row = make_edges(rows, cols, steps, n_il, n_dev)(u, r, s_il, w, part, sums, odd_sent, odd, w_got)
+        image, row = make_edges(rows, cols, steps, n_il, n_dev)(u, r, s_il, w, part, sums, g, odd, g_got)
         rows_all = lax.all_to_all(row, axes, 0, 0, tiled=True)
         return make_update(rows, cols, steps)(rows_all, x, r, u, image)
 

time: 26.1 us -> 26.8 us (1.027)
  local copies, waits for them, and re-layouts: 2.24 us -> 3.11 us
  starting transfers between devices: 5.2 us -> 4.74 us
    unnamed x12, local copies, waits for them, and re-layouts: 2.24 us -> 3.11 us
    ppermute x1, starting transfers between devices: 1.25 us -> 0.55 us  [step(): even = lax.ppermute(even_sent, axes, even_swap)]
where the time goes in v5:
time: 26.8 us; the launch traced here: 26.5 us
  blocking collectives  10.7 us (40%)
  starting transfers between devices  4.74 us (18%)
  waiting for transfers between devices  4.08 us (15%)
  local copies, waits for them, and re-layouts  3.11 us (12%)
  Pallas kernels  3.11 us (12%)
  between operations  0.71 us (3%)
    all_to_all x1, blocking collectives, step(): rows_all = lax.all_to_all(row, axes, 0, 0, tiled=True)  10.7 us
    unnamed x12, local copies, waits for them, and re-layouts  3.11 us
    ppermute x1, waiting for transfers between devices, step(): g_got = lax.ppermute(g, 'il', up)  2.88 us
    ppermute x1, starting transfers between devices, step(): odd = lax.ppermute(odd_sent, axes, odd_swap)  2.56 us
    ppermute x1, starting transfers between devices, step(): xl_got.append(lax.ppermute(buf, axes, xl_swaps[p][0]))  1.49 us
    pallas_call x1, Pallas kernels, step(): return make_update(rows, cols, steps)(rows_all, x, r, u, image)  1.36 us
    ppermute x1, waiting for transfers between devices, step(): xl_got.append(lax.ppermute(buf, axes, xl_swaps[p][0]))  1.19 us
    pallas_call x1, Pallas kernels, step(): part, sums = make_inner(rows, cols, steps)(u, r, s_il, s_xl, w)  1.04 us
  transfers between devices with their start and end apart: 4, of which 2 were waited for; matrix products, arithmetic and copies ran while one was open for 0% of the time, Pallas kernels for 5%

profile of v5, /device:TPU:0, one launch (start us, length us, event | category | flops | bytes accessed | tf_op | source)
XLA Modules:
  0.0 26.5 jit_solution(15730595357490030784)
XLA Ops:
  0.6 0.0 copy-start
  0.6 0.0 copy-start.1
  0.7 1.0 %copy-done = f32[4,64,512]{2,1,0:T(8,128)S(1)} copy-done((f32[4,64,512]{2,1,0:T(8,128)S(1)}, f32[4,64,512]{2,1,0:T(8,128)}, u32[]{:S(2)}) %copy-start) | copy-done | bytes 524312
  1.7 0.2 copy-done.1
  1.8 0.0 copy-start.4
  1.9 1.0 %copy-done.4 = f32[4,64,512]{2,1,0:T(8,128)S(1)} copy-done((f32[4,64,512]{2,1,0:T(8,128)S(1)}, f32[4,64,512]{2,1,0:T(8,128)}, u32[]{:S(2)}) %copy-start.4) | copy-done | bytes 524312
  2.9 0.1 pack.1._.rest_0_
  3.0 0.9 %copy-done.2 = f32[4,64,512]{2,1,0:T(8,128)S(1)} copy-done((f32[4,64,512]{2,1,0:T(8,128)S(1)}, f32[4,64,512]{2,1,0:T(8,128)}, u32[]{:S(2)}) %copy-start.2) | copy-done | bytes 524312
  3.9 0.1 pair.1.mine_ref
  4.1 0.5 %collective-permute-start = (f32[2,64,512]{2,1,0:T(8,128)S(1)}, f32[2,64,512]{2,1,0:T(8,128)S(1)}, u32[]{:S(2)}, u32[]{:S(2)}) collective-permute-start(f32[2,64,512]{2,1,0:T(8,128)S(1)} %pair.1.mine_ref), channel_id=1, source_target_pairs={{0,2},{1,3},{2,0},{3,1},{4,6},{5,7},{6,4},{7,5},{8,10},{9,11},{10,... | collective-permute-start | bytes 786440 | tf_op jit(solution)/shard_map/ppermute | solution.py:372
  4.6 2.6 %collective-permute-start.2 = (f32[64,512]{1,0:T(8,128)S(1)}, f32[64,512]{1,0:T(8,128)S(1)}, u32[]{:S(2)}, u32[]{:S(2)}) collective-permute-start(f32[64,512]{1,0:T(8,128)S(1)} %pick.1._), channel_id=1, source_target_pairs={{0,1},{1,0},{2,4},{3,5},{4,2},{5,3},{6,8},{7,9},{8,6},{9,7},{10,12... | collective-permute-start | bytes 393224 | tf_op jit(solution)/shard_map/ppermute | solution.py:366
  7.2 0.1 collective-permute-start.3
  7.3 1.5 %collective-permute-start.1 = (f32[8,512]{1,0:T(8,128)S(1)}, f32[8,512]{1,0:T(8,128)S(1)}, u32[]{:S(2)}, u32[]{:S(2)}) collective-permute-start(f32[8,512]{1,0:T(8,128)S(1)} %pack.1._.rest_0_), channel_id=1, source_target_pairs={{0,1},{2,3},{4,5},{6,7},{8,9},{10,11},{12,13},{14,15},{16,17},{18,... | collective-permute-start | bytes 49160 | tf_op jit(solution)/shard_map/ppermute | solution.py:370
  8.8 0.0 copy-done.3
  8.8 1.0 %inner.1 = (f32[4,64,512]{2,1,0:T(8,128)S(1)}, f32[4,8,512]{2,1,0:T(8,128)S(1)}) custom-call(f32[4,64,512]{2,1,0:T(8,128)S(1)} %copy-done, f32[4,64,512]{2,1,0:T(8,128)S(1)} %copy-done.3, f32[4,64,512]{2,1,0:T(8,128)S(1)} %copy-done.2, f32[4,64,512]{2,1,0:T(8,128)S(1)} %copy-done.4, f32[4,64,512]{2,1,0:T(8,128)S(1)} %copy-done.1), custom_call_target="tpu_custom_call" | custom-call | tf_op jit(solution)/shard_map/inner/pallas_call | solution.py:373
  9.9 1.2 %collective-permute-done.1.rest_1_ = f32[8,512]{1,0:T(8,128)S(1)} collective-permute-done((f32[8,512]{1,0:T(8,128)S(1)}, f32[8,512]{1,0:T(8,128)S(1)}, u32[]{:S(2)}, u32[]{:S(2)}) %collective-permute-start.1) | collective-permute-done | bytes 16416 | tf_op jit(solution)/shard_map/ppermute | solution.py:370
  11.1 0.0 collective-permute-done.got_ref
  11.1 0.3 %near_edges.1 = (f32[4,64,512]{2,1,0:T(8,128)S(1)}, f32[4,8,512]{2,1,0:T(8,128)S(1)}) custom-call(f32[4,64,512]{2,1,0:T(8,128)S(1)} %copy-done, f32[4,64,512]{2,1,0:T(8,128)S(1)} %copy-done.3, f32[4,64,512]{2,1,0:T(8,128)S(1)} %copy-done.2, f32[4,64,512]{2,1,0:T(8,128)S(1)} %copy-done.4, ...), custom_call_target="tpu_custom_call", output_to_operand_aliasing={{0}: (5, {}), {1}: (6, {})} | custom-call | tf_op jit(solution)/shard_map/near_edges/pallas_call | solution.py:374
  11.4 0.0 collective-permute-done.2.odd_ref
  11.4 2.9 %collective-permute-done.3.g_ref = f32[64,512]{1,0:T(8,128)S(1)} collective-permute-done((f32[64,512]{1,0:T(8,128)S(1)}, f32[64,512]{1,0:T(8,128)S(1)}, u32[]{:S(2)}, u32[]{:S(2)}) %collective-permute-start.3) | collective-permute-done | bytes 131104 | tf_op jit(solution)/shard_map/ppermute | solution.py:364
  14.3 0.1 edges.1
  14.4 10.7 %all_to_all.11 = f32[32,1,128]{2,1,0:T(1,128)S(1)} all-to-all(f32[32,1,128]{2,1,0:T(1,128)S(1)} %bitcast.5), channel_id=1, replica_groups=mesh['il'=16,'xl'=2] {'il','xl'}, dimensions={0} | all-to-all | bytes 32768 | tf_op jit(solution)/shard_map/all_to_all | solution.py:378
  25.1 0.0 copy-done.5
  25.1 1.4 %update.1 = (f32[4,64,512]{2,1,0:T(8,128)}, f32[4,64,512]{2,1,0:T(8,128)}, f32[4,64,512]{2,1,0:T(8,128)}) custom-call(f32[32,128]{1,0:T(8,128)S(1)} %bitcast.4, f32[4,64,512]{2,1,0:T(8,128)S(1)} %copy-done.5, f32[4,64,512]{2,1,0:T(8,128)S(1)} %copy-done.3, f32[4,64,512]{2,1,0:T(8,128)S(1)} %copy-done, f32[4,64,512]{2,1,0:T(8,128)S(1)} %get-tuple-element.14.img_ref), custom_call_target="tpu_custom_call" | custom-call | tf_op jit(solution)/shard_map/update/pallas_call | solution.py:379
  (5 shorter events, 0.1 us)
Async XLA Ops:
  0.6 1.0 %copy-start = (f32[4,64,512]{2,1,0:T(8,128)S(1)}, f32[4,64,512]{2,1,0:T(8,128)}, u32[]{:S(2)}) copy-start(f32[4,64,512]{2,1,0:T(8,128)} %u_ref.13) | copy-start | bytes 1572868
  0.6 1.2 %copy-start.1 = (f32[4,64,512]{2,1,0:T(8,128)S(1)}, f32[4,64,512]{2,1,0:T(8,128)}, u32[]{:S(2)}) copy-start(f32[4,64,512]{2,1,0:T(8,128)} %w_ref.11) | copy-start | bytes 1572868
  1.8 1.0 %copy-start.4 = (f32[4,64,512]{2,1,0:T(8,128)S(1)}, f32[4,64,512]{2,1,0:T(8,128)}, u32[]{:S(2)}) copy-start(f32[4,64,512]{2,1,0:T(8,128)} %sxl_ref.5) | copy-start | bytes 1572868
  2.9 1.0 %copy-start.2 = (f32[4,64,512]{2,1,0:T(8,128)S(1)}, f32[4,64,512]{2,1,0:T(8,128)}, u32[]{:S(2)}) copy-start(f32[4,64,512]{2,1,0:T(8,128)} %sil_ref.7) | copy-start | bytes 1572868
  3.9 4.9 %copy-start.3 = (f32[4,64,512]{2,1,0:T(8,128)S(1)}, f32[4,64,512]{2,1,0:T(8,128)}, u32[]{:S(2)}) copy-start(f32[4,64,512]{2,1,0:T(8,128)} %r_ref.7) | copy-start | bytes 1572868
  4.1 7.0 %collective-permute-start = (f32[2,64,512]{2,1,0:T(8,128)S(1)}, f32[2,64,512]{2,1,0:T(8,128)S(1)}, u32[]{:S(2)}, u32[]{:S(2)}) collective-permute-start(f32[2,64,512]{2,1,0:T(8,128)S(1)} %pair.1.mine_ref), channel_id=1, source_target_pairs={{0,2},{1,3},{2,0},{3,1},{4,6},{5,7},{6,4},{7,5},{8,10},{9,11},{10,... | collective-permute-start | bytes 786440 | tf_op jit(solution)/shard_map/ppermute | solution.py:372
  4.6 6.8 %collective-permute-start.2 = (f32[64,512]{1,0:T(8,128)S(1)}, f32[64,512]{1,0:T(8,128)S(1)}, u32[]{:S(2)}, u32[]{:S(2)}) collective-permute-start(f32[64,512]{1,0:T(8,128)S(1)} %pick.1._), channel_id=1, source_target_pairs={{0,1},{1,0},{2,4},{3,5},{4,2},{5,3},{6,8},{7,9},{8,6},{9,7},{10,12... | collective-permute-start | bytes 393224 | tf_op jit(solution)/shard_map/ppermute | solution.py:366
  7.2 7.1 %collective-permute-start.3 = (f32[64,512]{1,0:T(8,128)S(1)}, f32[64,512]{1,0:T(8,128)S(1)}, u32[]{:S(2)}, u32[]{:S(2)}) collective-permute-start(f32[64,512]{1,0:T(8,128)S(1)} %slope_row.1._.own_ref), channel_id=1, source_target_pairs={{0,2},{2,4},{4,6},{6,8},{8,10},{10,12},{12,14},{14,16},{16,18},{18... | collective-permute-start | bytes 393224 | tf_op jit(solution)/shard_map/ppermute | solution.py:364
  7.3 3.7 %collective-permute-start.1 = (f32[8,512]{1,0:T(8,128)S(1)}, f32[8,512]{1,0:T(8,128)S(1)}, u32[]{:S(2)}, u32[]{:S(2)}) collective-permute-start(f32[8,512]{1,0:T(8,128)S(1)} %pack.1._.rest_0_), channel_id=1, source_target_pairs={{0,1},{2,3},{4,5},{6,7},{8,9},{10,11},{12,13},{14,15},{16,17},{18,... | collective-permute-start | bytes 49160 | tf_op jit(solution)/shard_map/ppermute | solution.py:370
  14.3 10.9 %copy-start.5 = (f32[4,64,512]{2,1,0:T(8,128)S(1)}, f32[4,64,512]{2,1,0:T(8,128)}, u32[]{:S(2)}) copy-start(f32[4,64,512]{2,1,0:T(8,128)} %x_ref.1) | copy-start | bytes 1572868
